TPU v7x, 32 devices: a whole 2x2x4 slice. The times are simulated.
32 devices in a mesh: rows: 16 (over z, y, x), hid: 2 (over core).
Axes of the slice: x: 2, y: 2, z: 4, core: 2. Of those that a mesh axis runs over, the one named last changes fastest.
Arguments:
- tokens: bfloat16 [16384, 768], P('rows', 'hid'), may hold values from -8 to 8
- teacher: bfloat16 [16384, 768], P('rows', 'hid'), may hold values from -6 to 6
- segment_ids: int32 [32, 512], P('rows'), may hold values from 0 to 3, never falling along the last dimension, each value on 1 to 256 neighbouring positions
- valid_rows: int32 [32, 512], P('rows'), may hold values 0 or 1
- w_query: bfloat16 [768, 768], P(None, 'hid'), may hold values from -0.21875 to 0.21875
- b_query: bfloat16 [768], P('hid'), may hold values from -1.25 to 1.25
- w_key: bfloat16 [768, 768], P(None, 'hid'), may hold values from -0.21875 to 0.21875
- w_value: bfloat16 [768, 768], P(None, 'hid'), may hold values from -0.21875 to 0.21875
- b_value: bfloat16 [768], P('hid'), may hold values from -1.25 to 1.25
- w_out: bfloat16 [768, 768], P('hid'), may hold values from -1.25 to 1.25
- b_out: bfloat16 [768], P('hid'), may hold values from -1.25 to 1.25
- attention_norm_gain: bfloat16 [768], P('hid'), may hold values from 0.5 to 1.5
- first_shift: bfloat16 [768], P('hid'), may hold values from -1.25 to 1.25
- w_up: bfloat16 [768, 3072], P(None, 'hid'), may hold values from -0.21875 to 0.21875
- b_up: bfloat16 [3072], P('hid'), may hold values from -1.25 to 1.25
- w_down: bfloat16 [3072, 768], P('hid'), may hold values from -0.21875 to 0.21875
- b_down: bfloat16 [768], P('hid'), may hold values from -1.25 to 1.25
- feedforward_norm_gain: bfloat16 [768], P('hid'), may hold values from 0.5 to 1.5
- second_shift: bfloat16 [768], P('hid'), may hold values from -1.25 to 1.25
- head_alpha: float32 [12], P('hid'), may hold values from -1 to 3
- head_noise: float32 [12], P('hid'), may hold values from 0.05 to 0.95
- unit_alpha: float32 [3072], P('hid'), may hold values from -1 to 3
- unit_noise: float32 [3072], P('hid'), may hold values from 0.05 to 0.95
- hidden_alpha: float32 [768], P('hid'), may hold values from -1 to 3
- hidden_noise: float32 [768], P('hid'), may hold values from 0.05 to 0.95
- layer_alpha: float32 [2], replicated, may hold values from 0 to 3
- layer_noise: float32 [2], replicated, may hold values from 0.05 to 0.95
- hard_heads: int32 [12], P('hid'), may hold values 0 or 1
- hard_units: int32 [3072], P('hid'), may hold values 0 or 1
- hard_hidden: int32 [768], P('hid'), may hold values 0 or 1
Outputs:
- layer_out: bfloat16 [16384, 768], P('rows', 'hid')
- input_grad: float32 [16384, 768], P('rows', 'hid')
- w_query_grad: float32 [768, 768], P('rows', 'hid')
- b_query_grad: float32 [768], P('hid')
- w_key_grad: float32 [768, 768], P('rows', 'hid')
- w_value_grad: float32 [768, 768], P('rows', 'hid')
- b_value_grad: float32 [768], P('hid')
- w_out_grad: float32 [768, 768], P('hid', 'rows')
- b_out_grad: float32 [768], P('hid')
- first_gain_grad: float32 [768], P('hid')
- first_shift_grad: float32 [768], P('hid')
- w_up_grad: float32 [768, 3072], P('rows', 'hid')
- b_up_grad: float32 [3072], P('hid')
- w_down_grad: float32 [3072, 768], P('hid', 'rows')
- b_down_grad: float32 [768], P('hid')
- second_gain_grad: float32 [768], P('hid')
- second_shift_grad: float32 [768], P('hid')
- head_alpha_grad: float32 [12], P('hid')
- unit_alpha_grad: float32 [3072], P('hid')
- hidden_alpha_grad: float32 [768], P('hid')
- layer_alpha_grad: float32 [2], replicated
- hard_output: bfloat16 [16384, 768], P('rows', 'hid')
- hard_error: float32 [16384], P('rows')
Inputs may be any that keep to these rules, and one draw needn't show every extreme that they name: `segment_ids`: within a block the item numbers never fall.
All inputs are finite; a program needn't handle non-finite values. No bound on the sum of `valid_rows` or of `hard_heads` or of `hard_units` or of `hard_hidden` on one device may be relied on, other than what follows from the above.
Results may differ from a plain program's by a relative error of at most 0.015.
Values may be sent and summed in bfloat16 or wider, within the bound.
A program may use at most 128 MiB of HBM per device.

v0:
```python
import jax
import jax.numpy as jnp
from jax import lax
from jax.sharding import PartitionSpec as P

HEAD = 64


temper = 2.0 / 3.0
norm_eps = 1e-12
masked_score = -1e30


def gate_value(alpha, noise):
    return jax.nn.sigmoid((jnp.log(noise) - jnp.log(1.0 - noise) + alpha) / temper)


def gate_slope(value):
    return value * (1.0 - value) / temper


def product(left, right):
    return jnp.dot(left, right, preferred_element_type=jnp.float32)


def cross_rows(left, right):
    return lax.dot_general(
        left, right, (((0,), (0,)), ((), ())), preferred_element_type=jnp.float32
    )


def cross_cols(left, right):
    return lax.dot_general(
        left, right, (((1,), (1,)), ((), ())), preferred_element_type=jnp.float32
    )


def block_scores(query_block, key_block, segments, valid):
    length = segments.shape[0]
    diagonal = lax.broadcasted_iota(jnp.int32, (length, length), 0) == lax.broadcasted_iota(
        jnp.int32, (length, length), 1
    )
    allowed = (segments[:, None] == segments[None, :]) & (valid[None, :] > 0) | diagonal
    scores = jnp.einsum(
        "qhd,khd->hqk", query_block, key_block, preferred_element_type=jnp.float32
    ) * query_block.shape[-1] ** (-0.5)
    return jnp.where(allowed[None], scores, masked_score)


def attention_forward(query, keyed, value, segment_ids, valid_rows):

    def one_block(parts):
        query_block, key_block, value_block, segments, valid = parts
        scores = block_scores(query_block, key_block, segments, valid)
        highest = jnp.max(scores, -1, keepdims=True)
        raised = jnp.exp(scores - highest)
        totals = jnp.sum(raised, -1, keepdims=True)
        weights = (raised / totals).astype(jnp.bfloat16)
        context = jnp.einsum(
            "hqk,khd->qhd", weights, value_block, preferred_element_type=jnp.float32
        )
        return (context, (highest + jnp.log(totals))[..., 0])

    return lax.map(one_block, (query, keyed, value, segment_ids, valid_rows))


def attention_backward(query, keyed, value, segment_ids, valid_rows, logsum, dcontext):
    scale = query.shape[-1] ** (-0.5)

    def one_block(parts):
        query_block, key_block, value_block, segments, valid, logsum_block, dcontext_block = parts
        scores = block_scores(query_block, key_block, segments, valid)
        weights = jnp.exp(scores - logsum_block[..., None])
        dweights = jnp.einsum(
            "qhd,khd->hqk", dcontext_block, value_block, preferred_element_type=jnp.float32
        )
        dvalue = jnp.einsum(
            "hqk,qhd->khd",
            weights.astype(jnp.bfloat16),
            dcontext_block,
            preferred_element_type=jnp.float32,
        )
        balance = jnp.sum(weights * dweights, -1, keepdims=True)
        dscores = (weights * (dweights - balance)).astype(jnp.bfloat16)
        dquery = (
            jnp.einsum("hqk,khd->qhd", dscores, key_block, preferred_element_type=jnp.float32)
            * scale
        )
        dkeyed = (
            jnp.einsum("hqk,qhd->khd", dscores, query_block, preferred_element_type=jnp.float32)
            * scale
        )
        return (dquery, dkeyed, dvalue)

    return lax.map(one_block, (query, keyed, value, segment_ids, valid_rows, logsum, dcontext))


def layer_norm_forward(residual_state, norm_gain_value, norm_shift_value, retained_mask):
    model_width = residual_state.shape[1] * lax.axis_size("hid")
    sums = jnp.sum(residual_state, -1)
    squares = jnp.sum(residual_state * residual_state, -1)
    sums, squares = lax.psum((sums, squares), "hid")
    average_value = sums / model_width
    variance = squares / model_width - average_value * average_value
    inverse_deviation = lax.rsqrt(variance + norm_eps)
    centered_normalized = (residual_state - average_value[:, None]) * inverse_deviation[:, None]
    normalized_output = centered_normalized * norm_gain_value + norm_shift_value
    return (
        normalized_output * retained_mask,
        centered_normalized,
        inverse_deviation,
        normalized_output,
    )


def layer_norm_backward(
    incoming_gradient,
    centered_normalized,
    inverse_deviation,
    norm_gain_value,
    retained_mask,
    additional_term,
):
    model_width = incoming_gradient.shape[1] * lax.axis_size("hid")
    scaled_output = incoming_gradient * retained_mask
    normalized_grad = scaled_output * norm_gain_value
    attention_branch_sum = jnp.sum(normalized_grad, -1)
    feedforward_branch_sum = jnp.sum(normalized_grad * centered_normalized, -1)
    attention_branch_sum, feedforward_branch_sum, additional_sum = lax.psum(
        (attention_branch_sum, feedforward_branch_sum, additional_term), "hid"
    )
    residual_grad = inverse_deviation[:, None] * (
        normalized_grad
        - attention_branch_sum[:, None] / model_width
        - centered_normalized * feedforward_branch_sum[:, None] / model_width
    )
    return (
        residual_grad,
        jnp.sum(scaled_output * centered_normalized, 0),
        jnp.sum(scaled_output, 0),
        additional_sum,
    )


def shards(
    tokens,
    teacher,
    segment_ids,
    valid_rows,
    w_query,
    b_query,
    w_key,
    w_value,
    b_value,
    w_out,
    b_out,
    attention_norm_gain,
    first_shift,
    w_up,
    b_up,
    w_down,
    b_down,
    feedforward_norm_gain,
    second_shift,
    head_alpha,
    head_noise,
    unit_alpha,
    unit_noise,
    hidden_alpha,
    hidden_noise,
    layer_alpha,
    layer_noise,
    hard_heads,
    hard_units,
    hard_hidden,
):
    row_count, local_width = tokens.shape
    full_width = w_query.shape[0]
    block_count, block_rows = segment_ids.shape
    soft_heads = gate_value(head_alpha, head_noise)
    soft_units = gate_value(unit_alpha, unit_noise)
    relaxed_hidden_state = gate_value(hidden_alpha, hidden_noise)
    layer_gates = gate_value(layer_alpha, layer_noise)
    z_attn = layer_gates[0]
    z_ffn = layer_gates[1]
    head_count = local_width // HEAD
    tokens_float = tokens.astype(jnp.float32)
    target = teacher.astype(jnp.float32)
    piece = lax.all_gather(tokens, "hid", axis=1, tiled=True)
    query_sum = product(piece, w_query)
    key_sum = product(piece, w_key)
    value_sum = product(piece, w_value)
    whole_tokens = piece
    shaped = (block_count, block_rows, head_count, HEAD)
    query = (query_sum + b_query).astype(jnp.bfloat16).reshape(shaped)
    keyed = key_sum.astype(jnp.bfloat16).reshape(shaped)
    value = (value_sum + b_value).astype(jnp.bfloat16).reshape(shaped)
    context, logsum = attention_forward(query, keyed, value, segment_ids, valid_rows)
    context = context.reshape(row_count, head_count, HEAD)

    def take_hidden(piece):
        return (product(piece, w_up), piece)

    def layer_pass(z_head, z_unit, z_hidden, gate_attn, gate_ffn):
        mixed = (
            (context * z_head[None, :, None]).astype(jnp.bfloat16).reshape(row_count, local_width)
        )
        branch = lax.psum_scatter(product(mixed, w_out), "hid", scatter_dimension=1, tiled=True)
        residual_state = tokens_float + gate_attn * branch + b_out
        hidden_state, attention_centered, attention_inverse_deviation, attention_normalized = (
            layer_norm_forward(residual_state, attention_norm_gain, first_shift, z_hidden)
        )
        upper_sum, whole_hidden = take_hidden(
            lax.all_gather(hidden_state.astype(jnp.bfloat16), "hid", axis=1, tiled=True)
        )
        upper = upper_sum + b_up
        active = (jax.nn.gelu(upper, approximate=True) * z_unit).astype(jnp.bfloat16)
        down = lax.psum_scatter(
            product(active, w_down).astype(jnp.bfloat16), "hid", scatter_dimension=1, tiled=True
        ).astype(jnp.float32)
        resid_second = hidden_state + gate_ffn * down + b_down
        (
            final_output,
            feedforward_centered,
            feedforward_inverse_deviation,
            feedforward_normalized,
        ) = layer_norm_forward(resid_second, feedforward_norm_gain, second_shift, z_hidden)
        kept = (
            mixed,
            branch,
            attention_centered,
            attention_inverse_deviation,
            attention_normalized,
            whole_hidden,
            upper,
            active,
            down,
            feedforward_centered,
            feedforward_inverse_deviation,
            feedforward_normalized,
        )
        return (final_output, kept)

    final_output, kept = layer_pass(soft_heads, soft_units, relaxed_hidden_state, z_attn, z_ffn)
    (
        mixed,
        branch,
        attention_centered,
        attention_inverse_deviation,
        attention_normalized,
        whole_hidden,
        upper,
        active,
        down,
        feedforward_centered,
        feedforward_inverse_deviation,
        feedforward_normalized,
    ) = kept
    hard_final, unused = layer_pass(
        hard_heads.astype(jnp.float32),
        hard_units.astype(jnp.float32),
        hard_hidden.astype(jnp.float32),
        1.0,
        1.0,
    )
    error_portion = jnp.sum((hard_final - target) * (hard_final - target), -1)
    keep_rows = valid_rows.reshape(row_count, 1).astype(jnp.float32)
    final_output_grad = keep_rows * (final_output - target)
    dresid_second, second_gain_grad, second_shift_grad, error_sum = layer_norm_backward(
        final_output_grad,
        feedforward_centered,
        feedforward_inverse_deviation,
        feedforward_norm_gain,
        relaxed_hidden_state,
        error_portion,
    )
    hidden_dz = jnp.sum(final_output_grad * feedforward_normalized, 0)
    b_down_grad = jnp.sum(dresid_second, 0)
    feedforward_rows = jnp.sum(dresid_second * down, -1)
    ddown = (z_ffn * dresid_second).astype(jnp.bfloat16)
    piece = lax.all_gather(ddown, "hid", axis=1, tiled=True)
    dactive = cross_cols(piece, w_down)
    w_down_acc = cross_rows(active, piece)
    dactive, w_down_part = (dactive, w_down_acc)
    gelu_value, gelu_pull = jax.vjp(lambda entry: jax.nn.gelu(entry, approximate=True), upper)
    unit_dz = jnp.sum(dactive * gelu_value, 0)
    dupper = gelu_pull(dactive * soft_units)[0].astype(jnp.bfloat16)
    b_up_grad = jnp.sum(dupper.astype(jnp.float32), 0)
    w_up_part = cross_rows(whole_hidden, dupper)
    hidden_state_grad = dresid_second + lax.psum_scatter(
        cross_cols(dupper, w_up).astype(jnp.bfloat16), "hid", scatter_dimension=1, tiled=True
    ).astype(jnp.float32)
    dresid_first, first_gain_grad, first_shift_grad, ffn_sum = layer_norm_backward(
        hidden_state_grad,
        attention_centered,
        attention_inverse_deviation,
        attention_norm_gain,
        relaxed_hidden_state,
        feedforward_rows,
    )
    hidden_dz = hidden_dz + jnp.sum(hidden_state_grad * attention_normalized, 0)
    b_out_grad = jnp.sum(dresid_first, 0)
    attn_part = jnp.sum(dresid_first * branch)
    ffn_part = jnp.sum(ffn_sum) / lax.axis_size("hid")
    dbranch = (z_attn * dresid_first).astype(jnp.bfloat16)
    piece = lax.all_gather(dbranch, "hid", axis=1, tiled=True)
    dmixed = cross_cols(piece, w_out)
    w_out_acc = cross_rows(mixed, piece)
    dmixed, w_out_part = (dmixed, w_out_acc)
    dmixed = dmixed.reshape(row_count, head_count, HEAD)
    head_dz = jnp.sum(dmixed * context, (0, 2))
    dcontext = (dmixed * soft_heads[None, :, None]).astype(jnp.bfloat16).reshape(shaped)
    dquery, dkeyed, dvalue = attention_backward(
        query, keyed, value, segment_ids, valid_rows, logsum, dcontext
    )
    dquery = dquery.reshape(row_count, local_width).astype(jnp.bfloat16)
    dkeyed = dkeyed.reshape(row_count, local_width).astype(jnp.bfloat16)
    dvalue = dvalue.reshape(row_count, local_width).astype(jnp.bfloat16)
    b_query_grad = jnp.sum(dquery.astype(jnp.float32), 0)
    b_value_grad = jnp.sum(dvalue.astype(jnp.float32), 0)
    token_terms = (
        cross_cols(dquery, w_query) + cross_cols(dkeyed, w_key) + cross_cols(dvalue, w_value)
    )
    input_grad = dresid_first + lax.psum_scatter(
        token_terms.astype(jnp.bfloat16), "hid", scatter_dimension=1, tiled=True
    ).astype(jnp.float32)
    w_query_part = cross_rows(whole_tokens, dquery)
    w_key_part = cross_rows(whole_tokens, dkeyed)
    w_value_part = cross_rows(whole_tokens, dvalue)
    head_term = head_dz * gate_slope(soft_heads)
    unit_term = unit_dz * gate_slope(soft_units)
    hidden_term = hidden_dz * gate_slope(relaxed_hidden_state)
    layer_out = final_output.astype(jnp.bfloat16)
    hard_output = hard_final.astype(jnp.bfloat16)
    hard_error = error_sum / full_width
    w_query_grad, w_key_grad, w_value_grad, w_out_grad, w_up_grad, w_down_grad = (
        lax.psum_scatter(w_query_part, "rows", scatter_dimension=0, tiled=True),
        lax.psum_scatter(w_key_part, "rows", scatter_dimension=0, tiled=True),
        lax.psum_scatter(w_value_part, "rows", scatter_dimension=0, tiled=True),
        lax.psum_scatter(w_out_part, "rows", scatter_dimension=1, tiled=True),
        lax.psum_scatter(w_up_part, "rows", scatter_dimension=0, tiled=True),
        lax.psum_scatter(w_down_part, "rows", scatter_dimension=1, tiled=True),
    )
    summed = lax.psum(
        (
            b_query_grad,
            b_value_grad,
            b_out_grad,
            first_gain_grad,
            first_shift_grad,
            b_up_grad,
            b_down_grad,
            second_gain_grad,
            second_shift_grad,
            head_term,
            unit_term,
            hidden_term,
        ),
        "rows",
    )
    layer_sums = lax.psum(jnp.stack([attn_part, ffn_part]), ("rows", "hid"))
    layer_alpha_grad = layer_sums * gate_slope(layer_gates)
    return (
        layer_out,
        input_grad,
        w_query_grad,
        summed[0],
        w_key_grad,
        w_value_grad,
        summed[1],
        w_out_grad,
        summed[2],
        summed[3],
        summed[4],
        w_up_grad,
        summed[5],
        w_down_grad,
        summed[6],
        summed[7],
        summed[8],
        summed[9],
        summed[10],
        summed[11],
        layer_alpha_grad,
        hard_output,
        hard_error,
    )


def solution(mesh):
    in_specs = (
        P("rows", "hid"),
        P("rows", "hid"),
        P("rows", None),
        P("rows", None),
        P(None, "hid"),
        P("hid"),
        P(None, "hid"),
        P(None, "hid"),
        P("hid"),
        P("hid", None),
        P("hid"),
        P("hid"),
        P("hid"),
        P(None, "hid"),
        P("hid"),
        P("hid", None),
        P("hid"),
        P("hid"),
        P("hid"),
        P("hid"),
        P("hid"),
        P("hid"),
        P("hid"),
        P("hid"),
        P("hid"),
        P(),
        P(),
        P("hid"),
        P("hid"),
        P("hid"),
    )
    out_specs = (
        P("rows", "hid"),
        P("rows", "hid"),
        P("rows", "hid"),
        P("hid"),
        P("rows", "hid"),
        P("rows", "hid"),
        P("hid"),
        P("hid", "rows"),
        P("hid"),
        P("hid"),
        P("hid"),
        P("rows", "hid"),
        P("hid"),
        P("hid", "rows"),
        P("hid"),
        P("hid"),
        P("hid"),
        P("hid"),
        P("hid"),
        P("hid"),
        P(),
        P("rows", "hid"),
        P("rows"),
    )
    return jax.shard_map(shards, mesh=mesh, in_specs=in_specs, out_specs=out_specs, check_vma=False)
```

profile of v0, /device:TPU:0, one launch (start us, length us, event | category | flops | bytes accessed | tf_op | source)
XLA Modules:
  0.0 1163.0 jit_solution(13701738052297379410)
XLA Ops:
  10.2 11.9 %all-gather.6.cloned.1.call-done = bf16[1024,768]{1,0:T(8,128)(2,1)} async-done(((bf16[1024,384]{1,0:T(8,128)(2,1)}), bf16[1024,768]{1,0:T(8,128)(2,1)}) %all-gather.6.cloned.1.call-update) | async-done | bytes 1572880 | tf_op jit(solution)/shard_map/all_gather | solution.py:189
  47.3 45.5 %while.26 = (s32[]{:T(128)}, f32[2,512,6,64]{1,0,3,2:T(2,128)}, f32[2,6,512]{2,1,0:T(8,128)S(1)}, bf16[2,512,6,64]{1,3,2,0:T(8,128)(2,1)}, s32[2,512]{1,0:T(2,12...) while((s32[]{:T(128)}, f32[2,512,6,64]{1,0,3,2:T(2,128)}, ...), condition=%wide.region_3.4_spmd, body=%wide.region_0.3_spmd.sunk | while | flops 422573568 | bytes 25155712 | solution.py:64
  55.0 15.0 %dynamic_update_slice.27 = f32[2,512,6,64]{1,0,3,2:T(2,128)} dynamic-update-slice(f32[2,512,6,64]{1,0,3,2:T(2,128)} %get-tuple-element.556, f32[1,512,6,64]{1,0,3,2:T(1,128)S(1)} %copy.193, s32[]{:T(128)S(6)} %copy.202, s32[]{:T(128)} %constant.96.clone.1..sunk, s32[]{:T(128)} %constant.96.clone.1..sunk, s32[]{:T(128)} %constant.96.clone.1..sunk) | dynamic-update-slice | bytes 1572868 | tf_op jit(solution)/shard_map/while/body/jit(dynamic_update_index_in_dim)/dynamic_update_slice | solution.py:64
  77.8 15.0 %dynamic_update_slice.27 = f32[2,512,6,64]{1,0,3,2:T(2,128)} dynamic-update-slice(f32[2,512,6,64]{1,0,3,2:T(2,128)} %get-tuple-element.556, f32[1,512,6,64]{1,0,3,2:T(1,128)S(1)} %copy.193, s32[]{:T(128)S(6)} %copy.202, s32[]{:T(128)} %constant.96.clone.1..sunk, s32[]{:T(128)} %constant.96.clone.1..sunk, s32[]{:T(128)} %constant.96.clone.1..sunk) | dynamic-update-slice | bytes 1572868 | tf_op jit(solution)/shard_map/while/body/jit(dynamic_update_index_in_dim)/dynamic_update_slice | solution.py:64
  95.7 4.2 fusion.81
  100.8 4.3 fusion.97
  106.4 5.8 reduce-scatter.35.cloned.1.call-done
  112.2 14.4 %reduce-scatter.27.cloned.1.call-done = f32[1024,384]{1,0:T(8,128)} async-done(((f32[1024,768]{1,0:T(8,128)}), f32[1024,384]{1,0:T(8,128)}) %reduce-scatter.27.cloned.1.call-update) | async-done | bytes 1572880 | tf_op jit(solution)/shard_map/reduce_scatter | solution.py:208
  136.5 11.1 all-gather.14.cloned.1.call-done
  147.6 8.7 convolution_convert_fusion
  159.7 9.7 reduce-scatter.49.cloned.1.call-done
  171.6 5.0 fusion.101
  177.1 10.6 all-gather.8.cloned.1.call-done
  187.8 7.2 multiply_convert_fusion.1
  203.6 9.7 reduce-scatter.37.cloned.1.call-done
  220.9 5.5 multiply_reduce_fusion.6
  235.0 11.1 all-gather.10.cloned.1.call-done
  246.1 9.8 convert_reduce_fusion
  257.6 3.8 convolution_convert_fusion.1
  264.2 10.2 reduce-scatter.39.cloned.1.call-done
  283.0 3.8 multiply_reduce_fusion.4
  291.9 9.2 all-gather.12.cloned.1.call-done
  307.2 29.5 %while.27 = (s32[]{:T(128)}, bf16[2,512,6,64]{1,3,2,0:T(8,128)(2,1)S(1)}, bf16[2,512,6,64]{1,3,2,0:T(8,128)(2,1)}, bf16[2,512,6,64]{1,3,2,0:T(8,128)(2,1)}, bf16...) while((s32[]{:T(128)}, ...), condition=%wide.region_25.26_spmd, body=%wide.region_23.25_spmd.sunk | while | flops 1031665152 | bytes 53454984 | solution.py:95
  366.3 7.2 fusion.107
  374.9 6.2 fusion.106
  383.1 40.6 %psum.210 = f32[2]{0:T(128)S(1)} all-reduce(f32[2]{0:T(128)S(1)} %pad_maximum_fusion), channel_id=1, replica_groups=mesh['rows'=16,'hid'=2] {'rows','hid'}, use_global_device_ids=true, to_apply=%region_63.64 | all-reduce | flops 2 | bytes 16 | tf_op jit(solution)/shard_map/psum | solution.py:361
  426.7 76.2 %all-reduce = (f32[384]{0:T(512)}, f32[384]{0:T(512)}, f32[384]{0:T(512)}, f32[384]{0:T(512)}, f32[384]{0:T(512)}, /*index=5*/f32[1536]{0:T(1024)}, f32[384]{0:T...) all-reduce(f32[384]{0:T(512)S(1)} %reduce_sum.299, ...), channel_id=1, replica_groups=mesh['rows'=16,'hid'=2] {'rows'}, use_global_device_ids=true, to_apply=%region_29.30 | all-reduce | flops 6534 | bytes 52272 | tf_op jit(solution)/shard_map/psum | solution.py:344
  507.2 108.6 %reduce-scatter.43.cloned.1.call-done = f32[48,384]{1,0:T(8,128)} async-done(((f32[768,384]{1,0:T(8,128)}), f32[48,384]{1,0:T(8,128)}) %reduce-scatter.43.cloned.1.call-update) | async-done | bytes 73744
  615.8 127.9 %reduce-scatter.47.cloned.1.call-done = f32[48,384]{1,0:T(8,128)} async-done(((f32[768,384]{1,0:T(8,128)}), f32[48,384]{1,0:T(8,128)}) %reduce-scatter.47.cloned.1.call-update) | async-done | bytes 73744
  743.6 128.0 %reduce-scatter.45.cloned.1.call-done = f32[48,384]{1,0:T(8,128)} async-done(((f32[768,384]{1,0:T(8,128)}), f32[48,384]{1,0:T(8,128)}) %reduce-scatter.45.cloned.1.call-update) | async-done | bytes 73744
  871.7 142.1 %reduce-scatter.33.cloned.1.call-done = f32[1536,48]{0,1:T(8,128)} async-done(((f32[1536,768]{0,1:T(8,128)}), f32[1536,48]{0,1:T(8,128)}) %reduce-scatter.33.cloned.1.call-update) | async-done | bytes 294928 | tf_op jit(solution)/shard_map/reduce_scatter | solution.py:342
  1013.8 142.3 %reduce-scatter.31.cloned.1.call-done = f32[48,1536]{1,0:T(8,128)} async-done(((f32[768,1536]{1,0:T(8,128)}), f32[48,1536]{1,0:T(8,128)}) %reduce-scatter.31.cloned.1.call-update) | async-done | bytes 294928 | tf_op jit(solution)/shard_map/reduce_scatter | solution.py:341
  (260 shorter events, 182.2 us)
Async XLA Ops:
  7.2 140.4 %copy-start = (bf16[768,1536]{1,0:T(8,128)(2,1)S(1)}, bf16[768,1536]{1,0:T(8,128)(2,1)}, u32[]{:S(2)}) copy-start(bf16[768,1536]{1,0:T(8,128)(2,1)} %param.47) | copy-start | bytes 7077892
  7.2 14.9 %all-gather.6.cloned.1.call-start = ((), (), s32[]{:S(2)}) async-start(), calls=%async_computation.12 | async-start | bytes 2359296 | tf_op jit(solution)/shard_map/all_gather | solution.py:189
  7.9 104.3 %reduce-scatter.35.cloned.1.call-start = ((), (), s32[]{:S(2)}) async-start(), calls=%async_computation.20 | async-start | bytes 4718592 | tf_op jit(solution)/shard_map/reduce_scatter | solution.py:208
  43.7 3.6 copy-start.18
  43.7 3.6 copy-start.19
  92.8 3.0 copy-start.7
  99.9 26.7 %reduce-scatter.27.cloned.1.call-start = ((), (), s32[]{:S(2)}) async-start(), calls=%async_computation.13 | async-start | bytes 4718592 | tf_op jit(solution)/shard_map/reduce_scatter | solution.py:208
  100.7 4.3 copy-start.20
  105.1 21.6 %copy-start.5 = (bf16[1024,384]{1,0:T(8,128)(2,1)S(1)}, bf16[1024,384]{1,0:T(8,128)(2,1)}, u32[]{:S(2)}) copy-start(bf16[1024,384]{1,0:T(8,128)(2,1)} %param.34) | copy-start | bytes 2359300
  105.1 42.5 %all-gather.14.cloned.1.call-start = ((), (), s32[]{:S(2)}) async-start(), calls=%async_computation.21 | async-start | bytes 2359296 | tf_op jit(solution)/shard_map/all_gather | solution.py:214
  105.8 20.9 %copy-start.29 = (f32[2]{0:T(128)}, f32[2]{0:T(128)S(1)}, u32[]{:S(2)}) copy-start(f32[2]{0:T(128)S(1)} %add_divide_fusion.3) | copy-start | bytes 28
  136.4 32.9 %reduce-scatter.49.cloned.1.call-start = ((), (), s32[]{:S(2)}) async-start(), calls=%async_computation.28 | async-start | bytes 2359296
  159.0 28.8 %all-gather.8.cloned.1.call-start = ((), (), s32[]{:S(2)}) async-start(), calls=%async_computation.14 | async-start | bytes 2359296 | tf_op jit(solution)/shard_map/all_gather | solution.py:214
  171.6 5.5 copy-start.22
  171.6 5.5 copy-start.23
  176.6 36.7 %reduce-scatter.37.cloned.1.call-start = ((), (), s32[]{:S(2)}) async-start(), calls=%async_computation.22 | async-start | bytes 2359296
  187.8 8.9 copy-start.37
  203.0 43.1 %all-gather.10.cloned.1.call-start = ((), (), s32[]{:S(2)}) async-start(), calls=%async_computation.15 | async-start | bytes 2359296 | tf_op jit(solution)/shard_map/all_gather | solution.py:281
  234.9 39.5 %reduce-scatter.39.cloned.1.call-start = ((), (), s32[]{:S(2)}) async-start(), calls=%async_computation.23 | async-start | bytes 2359296
  263.9 12.8 %copy-start.2 = (f32[1024,384]{1,0:T(8,128)S(1)}, f32[1024,384]{1,0:T(8,128)}, u32[]{:S(2)}) copy-start(f32[1024,384]{1,0:T(8,128)} %get-tuple-element.404) | copy-start | bytes 4718596
  263.9 12.8 %copy-start.4 = (f32[1024,384]{1,0:T(8,128)S(1)}, f32[1024,384]{1,0:T(8,128)}, u32[]{:S(2)}) copy-start(f32[1024,384]{1,0:T(8,128)} %copy-done.3) | copy-start | bytes 4718596
  264.0 37.1 %all-gather.12.cloned.1.call-start = ((), (), s32[]{:S(2)}) async-start(), calls=%async_computation.16 | async-start | bytes 2359296 | tf_op jit(solution)/shard_map/all_gather | solution.py:306
  290.0 212.9 %reduce-scatter.41.cloned.1.call-start = ((), (), s32[]{:S(2)}) async-start(), calls=%async_computation.24 | async-start | bytes 2359296
  338.9 3.3 copy-start.10
  347.4 159.8 %reduce-scatter.29.cloned.1.call-start = ((), (), s32[]{:S(2)}) async-start(), calls=%async_computation.17 | async-start | bytes 1253376 | tf_op jit(solution)/shard_map/reduce_scatter | solution.py:340
  352.3 263.4 %reduce-scatter.43.cloned.1.call-start = ((), (), s32[]{:S(2)}) async-start(), calls=%async_computation.25 | async-start | bytes 1253376
  356.2 387.4 %reduce-scatter.47.cloned.1.call-start = ((), (), s32[]{:S(2)}) async-start(), calls=%async_computation.27 | async-start | bytes 1253376
  362.4 509.3 %reduce-scatter.45.cloned.1.call-start = ((), (), s32[]{:S(2)}) async-start(), calls=%async_computation.26 | async-start | bytes 1253376
  366.0 647.8 %reduce-scatter.33.cloned.1.call-start = ((), (), s32[]{:S(2)}) async-start(), calls=%async_computation.19 | async-start | bytes 5013504 | tf_op jit(solution)/shard_map/reduce_scatter | solution.py:342
  373.5 782.5 %reduce-scatter.31.cloned.1.call-start = ((), (), s32[]{:S(2)}) async-start(), calls=%async_computation.18 | async-start | bytes 5013504 | tf_op jit(solution)/shard_map/reduce_scatter | solution.py:341
  381.1 42.6 %copy-start.30 = (f32[2]{0:T(128)S(1)}, f32[2]{0:T(128)}, u32[]{:S(2)}) copy-start(f32[2]{0:T(128)} %copy-done.29) | copy-start | bytes 28
  502.9 653.2 %copy-start.1 = (bf16[768,1536]{1,0:T(8,128)(2,1)S(1)}, bf16[768,1536]{1,0:T(8,128)(2,1)}, u32[]{:S(2)}) copy-start(bf16[768,1536]{1,0:T(8,128)(2,1)} %param.47) | copy-start | bytes 7077892
  (28 other events, 34.3 us)
Sparse Core Ops, SparseCore 0:
  9.6 12.4 all-gather.5
  100.1 12.0 reduce-scatter.34
  114.5 12.0 reduce-scatter.26
  136.5 11.0 all-gather.13
  159.1 10.1 reduce-scatter.48
  176.7 10.9 all-gather.7
  203.1 10.2 reduce-scatter.36
  235.0 10.9 all-gather.9
  264.1 10.2 reduce-scatter.38
  290.1 10.9 all-gather.11
  347.5 10.2 reduce-scatter.40
  363.0 124.8 reduce-scatter.28
  493.2 122.5 reduce-scatter.42
  620.9 122.6 reduce-scatter.46
  748.8 122.8 reduce-scatter.44
  877.3 136.4 reduce-scatter.32
  1020.2 135.8 reduce-scatter.30
where the time goes:
time: 1180 us; the launch traced here: 1160 us
  waiting for transfers between devices  754 us (64%)
  blocking collectives  129 us (11%)
  matrix products  117 us (10%)
  local copies, waits for them, and re-layouts  93.7 us (8%)
  other arithmetic  51.5 us (4%)
  between operations  15.6 us (1%)
    unnamed x24, waiting for transfers between devices  395 us
    reduce_scatter x1, waiting for transfers between devices, shards(): lax.psum_scatter(w_up_part, 'rows', scatter_dimension=0, tiled=True)  142 us
    reduce_scatter x1, waiting for transfers between devices, shards(): lax.psum_scatter(w_down_part, 'rows', scatter_dimension=1, tiled=True)  142 us
    psum x1, blocking collectives, shards(): lax.psum((b_query_grad, b_value_grad, b_out_grad, first_gain_grad, first_...  76.2 us
    psum x1, blocking collectives, shards(): layer_sums = lax.psum(jnp.stack([attn_part, ffn_part]), ('rows', 'hid'))  40.6 us
    dot_general x8, matrix products, product(): return jnp.dot(left, right, preferred_element_type=jnp.float32)  38.1 us
    unnamed x102, local copies, waits for them, and re-layouts  37.1 us
    dynamic_update_slice x4, local copies, waits for them, and re-layouts, attention_forward(): return lax.map(one_block, (query, keyed, value, segment_ids, valid_rows))  31.6 us
  transfers between devices with their start and end apart: 17, of which 15 were waited for; matrix products, arithmetic and copies ran while one was open for 4% of the time, Pallas kernels for 0%

commit v1 on v0

v1 whole, which is shorter than its diff:
```python
import functools

import jax
import jax.numpy as jnp
from jax import lax
from jax.experimental import pallas as pl
from jax.experimental.pallas import tpu as pltpu
from jax.sharding import PartitionSpec as P

HEAD = 64
f32 = jnp.float32
bf16 = jnp.bfloat16
MESH = pl.DeviceIdType.MESH

temper = 2.0 / 3.0
norm_eps = 1e-12
masked_score = -1e30

PB_Q, PB_V, PB_O, PG1, PS1, PB_D, PG2, PS2, PZH, PHH, PZHEAD, PHHEAD, PZA, PZF = range(14)
S_BQ, S_BV, S_BO, S_G1, S_S1, S_BD, S_G2, S_S2, S_ZH, S_ZHEAD, S_ZA, S_ZF = range(12)
X_TOK, X_HID, X_DDOWN = range(3)
X_DBR = X_DDOWN


def gate_value(alpha, noise):
    return jax.nn.sigmoid((jnp.log(noise) - jnp.log(1.0 - noise) + alpha) / temper)


def mm(a, b):
    return lax.dot_general(a, b, (((1,), (0,)), ((), ())), preferred_element_type=f32)


def mm_nt(a, b):
    return lax.dot_general(a, b, (((1,), (1,)), ((), ())), preferred_element_type=f32)


def loop(count, body):
    def step(i, carry):
        body(i)
        return carry

    lax.fori_loop(0, count, step, 0)


def al(x, m):
    return pl.multiple_of(x, m)


def layer_kernel(dims, *refs):
    n, D, F, M, use_rs = dims
    DH, FH = D // 2, F // 2
    heads = D // HEAD
    pairs = heads // 2
    groups = 4 + 2 * (FH // DH)
    fgroups = FH // DH
    (
        tok_h,
        tea_h,
        seg_ref,
        valid_ref,
        wq_h,
        wk_h,
        wv_h,
        wout_h,
        wup_h,
        wdown_h,
        pd_h,
        pf_h,
    ) = refs[:12]
    count = 8 if use_rs else 6
    outs = refs[12 : 12 + count]
    layer_out_h, input_grad_h, hard_out_h, err_out, vec_out = outs[:5]
    (
        tok,
        tea,
        wqkv,
        wout,
        wup,
        wdown,
        pd,
        pf,
        qkv,
        qkv_peer,
        bias,
        probs,
        ctx,
        mixed,
        mixed_peer,
        resid,
        hbf,
        acc,
        act,
        act_peer,
        gp,
        dup_peer,
        dres,
        dbf,
        xt,
        vd,
        vf,
        pack,
        packr,
        packs,
        errs,
        G,
        recv1,
        recv2,
        recv3,
        lsem,
        ssem,
        rsem,
        xs,
        xr,
        s1,
        r1,
        s2,
        r2,
        s3,
        r3,
        credit,
    ) = refs[12 + count :]

    r = lax.axis_index("rows")
    h = lax.axis_index("hid")
    oh = 1 - h
    peer = (r, oh)
    x = lax.rem(r, 2)
    y = lax.rem(lax.div(r, 2), 2)
    z = lax.div(r, 4)
    zc = n // 4

    def chip(cx, cy, cz):
        return (cz * 4 + cy * 2 + cx, h)

    barrier = pltpu.get_barrier_semaphore()
    partners = [peer]
    if use_rs:
        partners += [chip(1 - x, y, z), chip(x, 1 - y, z), chip(1 - x, 1 - y, z)]
        partners += [chip(x, y, lax.rem(z + d, zc)) for d in range(1, zc)]
    for p in partners:
        pl.semaphore_signal(barrier, inc=1, device_id=p, device_id_type=MESH)
    pl.semaphore_wait(barrier, len(partners))

    cols = pl.ds(al(h * DH, 128), DH)
    ocols = pl.ds(al(oh * DH, 128), DH)
    fcols = pl.ds(al(h * FH, 128), FH)
    ofcols = pl.ds(al(oh * FH, 128), FH)
    mine = pl.ds(al(h * M, 128), M)
    other = pl.ds(al(oh * M, 128), M)
    feeds = [
        (pd_h, pd_h, pd.at[:, cols]),
        (pf_h, pf_h, pf.at[:, fcols]),
        (tok_h.at[mine], tok_h.at[other], tok.at[:, cols]),
        (wq_h, wq_h, wqkv.at[:, pl.ds(al(h * DH, 128), DH)]),
        (wk_h, wk_h, wqkv.at[:, pl.ds(al(h * DH + D, 128), DH)]),
        (wv_h, wv_h, wqkv.at[:, pl.ds(al(h * DH + 2 * D, 128), DH)]),
        (wout_h, wout_h, wout.at[cols]),
        (wup_h, wup_h, wup.at[:, fcols]),
        (wdown_h, wdown_h, wdown.at[fcols]),
        (tea_h.at[mine], tea_h.at[other], tea.at[:, cols]),
    ]
    local = []
    remote = []
    for i, (src, src_other, dst) in enumerate(feeds):
        far = pltpu.make_async_remote_copy(
            src_ref=src_other,
            dst_ref=dst,
            send_sem=ssem.at[i],
            recv_sem=rsem.at[i],
            device_id=peer,
            device_id_type=MESH,
        )
        far.start()
        near = pltpu.make_async_copy(src, dst, lsem.at[i])
        near.start()
        local.append(near)
        remote.append(far)

    def fed(*which):
        for i in which:
            local[i].wait()
            remote[i].wait_recv()

    def to_peer(k, src, dst):
        copy = pltpu.make_async_remote_copy(
            src_ref=src,
            dst_ref=dst,
            send_sem=xs.at[k],
            recv_sem=xr.at[k],
            device_id=peer,
            device_id_type=MESH,
        )
        copy.start()
        return copy

    def far_copy(src, dst, send, recv, device):
        return pltpu.make_async_remote_copy(
            src_ref=src,
            dst_ref=dst,
            send_sem=send,
            recv_sem=recv,
            device_id=device,
            device_id_type=MESH,
        )

    def send1(g, first):
        if first == 0:
            return far_copy(G.at[g, :, :, 1 - x], recv1.at[g], s1.at[g], r1.at[g], chip(1 - x, y, z))
        return far_copy(G.at[g, :, 1 - y], recv1.at[g], s1.at[g], r1.at[g], chip(x, 1 - y, z))

    def send2(g, first):
        if first == 0:
            return far_copy(
                G.at[g, :, 1 - y, x], recv2.at[g], s2.at[g], r2.at[g], chip(x, 1 - y, z)
            )
        return far_copy(G.at[g, :, y, 1 - x], recv2.at[g], s2.at[g], r2.at[g], chip(1 - x, y, z))

    def send3(g, d):
        to = lax.rem(z + d, zc)
        return far_copy(
            G.at[g, to, y, x], recv3.at[g, d - 1], s3.at[g, d - 1], r3.at[g, d - 1], chip(x, y, to)
        )

    def stage1(g, first):
        send1(g, first).wait_recv()

        def body(k):
            for j in range(2):
                if first == 0:
                    at = G.at[g, k, j, x]
                else:
                    at = G.at[g, k, y, j]
                at[...] = (at[...].astype(f32) + recv1[g, k, j].astype(f32)).astype(bf16)

        loop(zc, body)
        send2(g, first).start()

    def stage2(g, first):
        send2(g, first).wait_recv()

        def body(k):
            at = G.at[g, k, y, x]
            at[...] = (at[...].astype(f32) + recv2[g, k].astype(f32)).astype(bf16)

        loop(zc, body)
        for d in range(1, zc):
            send3(g, d).start()

    def final(g):
        for d in range(1, zc):
            send3(g, d).wait_recv()
        total = G[g, z, y, x].astype(f32)
        for d in range(1, zc):
            total = total + recv3[g, d - 1].astype(f32)
        return total

    npairs = groups // 2

    def tick(i):
        if not use_rs:
            return

        @pl.when(i < npairs)
        def _():
            for b in range(2):
                stage1(2 * i + b, b)

        @pl.when((i >= 1) & (i < npairs + 1))
        def _():
            for b in range(2):
                stage2(2 * i - 2 + b, b)

    RT = 64

    def row_loop(body):
        loop(M // RT, lambda i: body(pl.ds(al(i * RT, RT), RT)))

    def add_sum(k, value):
        at = vd.at[pl.ds(8 * k, 8)]
        at[...] = at[...] + jnp.sum(value.reshape(RT // 8, 8, D), axis=0)

    def par(k):
        return pd[pl.ds(k, 1), :]

    def normed(resid_tile):
        mean = jnp.sum(resid_tile, -1, keepdims=True) / D
        var = jnp.sum(resid_tile * resid_tile, -1, keepdims=True) / D - mean * mean
        inv = lax.rsqrt(var + norm_eps)
        return (resid_tile - mean) * inv, inv

    dctx = outb = hbf

    def transpose_to(src, k, sem):
        def body(i):
            at = pl.ds(al(i * 128, 128), 128)
            xt[k, :, at] = src[at, :].T

        loop(M // 128, body)
        return to_peer(sem, xt.at[k, :, pl.ds(0, M)], xt.at[k, :, pl.ds(M, M)])

    NT = 256

    def tiles(count, body):
        loop(count // NT, lambda i: body(pl.ds(al(i * NT, NT), NT)))

    def project_out(gate):
        def body(at):
            acc[:, at] = mm(mixed[...], wout[:, at])

        tiles(D, body)

        def rows_body(at):
            value = tok[at, :].astype(f32) + acc[at, :] * gate + par(PB_O)
            resid[at, :] = value

        row_loop(rows_body)

    def first_norm(mask):
        def body(at):
            xh, inv = normed(resid[at, :])
            hbf[at, :] = ((xh * par(PG1) + par(PS1)) * par(mask)).astype(bf16)

        row_loop(body)

    def up(unit_row, keep):
        def body(at):
            u = mm(hbf[...], wup[:, at]) + pf[pl.ds(0, 1), at]
            u2 = u * u
            half = 0.5 * jnp.tanh(u * (0.7978845608 + (0.7978845608 * 0.044715) * u2)) + 0.5
            act[:, at] = (u * half * pf[pl.ds(unit_row, 1), at]).astype(bf16)
            if keep:
                slope = half + u * (2.0 * half * (1.0 - half)) * (
                    0.7978845608 + (3.0 * 0.7978845608 * 0.044715) * u2
                )
                gp[:, at] = slope.astype(bf16)

        tiles(F, body)

    def down():
        def body(at):
            acc[:, at] = mm(act[...], wdown[:, at])

        tiles(D, body)

    row_seg = seg_ref[pl.ds(h, 1), :].astype(f32)
    row_valid = valid_ref[pl.ds(h, 1), :].astype(f32)
    col_seg = jnp.broadcast_to(row_seg, (128, M)).T[:, :1]
    col_valid = jnp.broadcast_to(row_valid, (128, M)).T
    errs[...] = jnp.zeros_like(errs)
    vd[...] = jnp.zeros_like(vd)
    diagonal = lax.broadcasted_iota(jnp.int32, (M, M), 0) == lax.broadcasted_iota(
        jnp.int32, (M, M), 1
    )
    allowed = ((col_seg == row_seg) & (row_valid > 0)) | diagonal
    bias[...] = jnp.where(allowed, 0.0, masked_score).astype(bf16)
    keep_ref = errs
    keep_ref[...] = col_valid

    fed(0, 1, 2, 3, 4, 5)

    for part, row in ((0, PB_Q), (1, None), (2, PB_V)):

        def body(i, part=part, row=row):
            at = pl.ds(al(i * NT, NT), NT)
            wide = pl.ds(al(i * NT + part * D, NT), NT)
            value = mm(tok[...], wqkv[:, wide])
            if row is not None:
                value = value + pd[pl.ds(row, 1), at]
            value = value.astype(bf16)
            if part == 0:
                value = value * jnp.asarray(HEAD**-0.5, bf16)
            qkv[:, wide] = value

        loop(D // NT, body)

    tok_copy = transpose_to(tok, X_TOK, 0)

    lane = lax.broadcasted_iota(jnp.int32, (1, 2 * HEAD), 1)
    head_mask = [(lane < HEAD).astype(bf16), (lane >= HEAD).astype(bf16)]

    QT = 256

    def attend(i):
        p = lax.div(i, M // QT)
        rows = pl.ds(al(lax.rem(i, M // QT) * QT, QT), QT)
        at = pl.ds(al(p * 128, 128), 128)
        q2 = qkv[rows, at]
        k2 = qkv[:, pl.ds(al(p * 128 + D, 128), 128)]
        v2 = qkv[:, pl.ds(al(p * 128 + 2 * D, 128), 128)]
        total = None
        for b in range(2):
            s = mm_nt(q2 * head_mask[b], k2) + bias[rows, :].astype(f32)
            e = jnp.exp(s - jnp.max(s, -1, keepdims=True))
            w = (e * (1.0 / jnp.sum(e, -1, keepdims=True))).astype(bf16)
            probs[2 * p + b, rows] = w
            part = mm(w, v2 * head_mask[b])
            total = part if total is None else total + part
        ctx[rows, at] = total.astype(bf16)
        mixed[rows, at] = (total * pd[pl.ds(PZHEAD, 1), at]).astype(bf16)

    loop(pairs * (M // QT), attend)
    mixed_copy = to_peer(4, mixed.at[:, ocols], mixed_peer)

    fed(6)
    project_out(par(PZA))
    first_norm(PZH)
    hid_copy = transpose_to(hbf, X_HID, 1)
    fed(7)
    up(1, True)
    act_copy = to_peer(5, act.at[:, ofcols], act_peer)
    fed(8, 9)
    down()

    def second_norm(at):
        xh1, inv1 = normed(resid[at, :])
        hidden = (xh1 * par(PG1) + par(PS1)) * par(PZH)
        dn = acc[at, :]
        xh, inv = normed(hidden + par(PZF) * dn + par(PB_D))
        nrm = xh * par(PG2) + par(PS2)
        fin = nrm * par(PZH)
        outb[at, :] = fin.astype(bf16)
        d = keep_ref[at, :][:, :1] * (fin - tea[at, :].astype(f32))
        dz = d * par(PZH)
        add_sum(S_S2, dz)
        add_sum(S_G2, dz * xh)
        add_sum(S_ZH, d * nrm)
        e = dz * par(PG2)
        dr = inv * (
            e - jnp.sum(e, -1, keepdims=True) / D - xh * (jnp.sum(e * xh, -1, keepdims=True) / D)
        )
        add_sum(S_BD, dr)
        add_sum(S_ZF, dr * dn)
        dres[at, :] = dr
        dbf[at, :] = (dr * par(PZF)).astype(bf16)

    row_loop(second_norm)
    out_near = pltpu.make_async_copy(outb.at[:, cols], layer_out_h.at[mine], lsem.at[10])
    out_near.start()
    out_far = to_peer(6, outb.at[:, ocols], layer_out_h.at[mine])

    ddown_copy = transpose_to(dbf, X_DDOWN, 2)

    def dactive_tile(at):
        da = mm_nt(dbf[...], wdown[at, :])
        su = jnp.sum((da * act[:, at].astype(f32)).reshape(M // 8, 8, NT), axis=0)
        vf[pl.ds(8, 8), at] = su
        du = (da * pf[pl.ds(1, 1), at] * gp[:, at].astype(f32)).astype(bf16)
        gp[:, at] = du
        vf[pl.ds(0, 8), at] = jnp.sum(du.astype(f32).reshape(M // 8, 8, NT), axis=0)

    tiles(F, dactive_tile)
    dup_copy = to_peer(7, gp.at[:, ofcols], dup_peer)

    GT = D // 4

    def grad_group(g, k, own, own_at, far, far_at):
        def body(i):
            at = pl.ds(al(i * GT, GT), GT)
            value = mm(xt[k, at, pl.ds(0, M)], own[:, own_at]) + mm(
                xt[k, at, pl.ds(M, M)], far[:, far_at]
            )
            if use_rs:
                G[g, i] = value.astype(bf16).reshape(2, 2, D // n, DH)
            else:
                G[g, at] = value.astype(bf16)

        loop(4, body)

    def start1(g, first):
        if use_rs:
            send1(g, first).start()

    ddown_copy.wait_recv()
    act_copy.wait_recv()

    def down_grad(i):
        for b in range(2):
            g = 2 * i + b
            grad_group(
                g,
                X_DDOWN,
                act,
                pl.ds(al(h * FH + g * DH, 128), DH),
                act_peer,
                pl.ds(al(g * DH, 128), DH),
            )
            start1(g, b)

    loop(fgroups // 2, down_grad)
    pl.semaphore_signal(credit, inc=1, device_id=peer, device_id_type=MESH)

    def dhidden_tile(at):
        acc[:, at] = mm_nt(gp[...], wup[at, :])

    tiles(D, dhidden_tile)

    hid_copy.wait_recv()
    dup_copy.wait_recv()

    def up_grad(i):
        for b in range(2):
            g = 2 * i + b
            grad_group(
                g + fgroups,
                X_HID,
                gp,
                pl.ds(al(h * FH + g * DH, 128), DH),
                dup_peer,
                pl.ds(al(g * DH, 128), DH),
            )
            start1(g + fgroups, b)

    loop(fgroups // 2, up_grad)

    def first_norm_back(at):
        value = resid[at, :]
        xh, inv = normed(value)
        dh = dres[at, :] + acc[at, :]
        dz = dh * par(PZH)
        add_sum(S_S1, dz)
        add_sum(S_G1, dz * xh)
        add_sum(S_ZH, dh * (xh * par(PG1) + par(PS1)))
        e = dz * par(PG1)
        dr = inv * (
            e - jnp.sum(e, -1, keepdims=True) / D - xh * (jnp.sum(e * xh, -1, keepdims=True) / D)
        )
        add_sum(S_BO, dr)
        add_sum(S_ZA, dr * (value - tok[at, :].astype(f32) - par(PB_O)))
        dres[at, :] = dr
        dbf[at, :] = (dr * par(PZA)).astype(bf16)

    row_loop(first_norm_back)
    tick(0)
    out_near.wait()
    out_far.wait_send()
    ddown_copy.wait_send()
    pl.semaphore_wait(credit, 1)
    dbr_copy = transpose_to(dbf, X_DBR, 3)

    def dmixed_tile(at):
        dm = mm_nt(dbf[...], wout[at, :])
        vd[pl.ds(8 * S_ZHEAD, 8), at] = jnp.sum(
            (dm * ctx[:, at].astype(f32)).reshape(M // 8, 8, NT), axis=0
        )
        dctx[:, at] = (dm * pd[pl.ds(PZHEAD, 1), at]).astype(bf16)

    tiles(D, dmixed_tile)
    dbr_copy.wait_recv()
    mixed_copy.wait_recv()
    g_out = 2 * fgroups
    grad_group(g_out, X_DBR, mixed, cols, mixed_peer, pl.ds(0, DH))
    start1(g_out, 0)

    qkv_copies = [
        far_copy(
            qkv.at[:, pl.ds(al(oh * DH + j * D, 128), DH)],
            qkv_peer.at[:, pl.ds(j * DH, DH)],
            xs.at[9 + j],
            xr.at[9 + j],
            peer,
        )
        for j in range(3)
    ]
    scale = HEAD**-0.5

    def attend_back(i):
        p = lax.rem(oh * (pairs // 2) + i, pairs)
        qa = pl.ds(al(p * 128, 128), 128)
        ka = pl.ds(al(p * 128 + D, 128), 128)
        va = pl.ds(al(p * 128 + 2 * D, 128), 128)
        k2, v2 = qkv[:, ka], qkv[:, va]
        dkt = dvt = None
        parts = []
        for t in range(M // QT):
            rows = pl.ds(t * QT, QT)
            q2, c2 = qkv[rows, qa], dctx[rows, qa]
            dq = None
            for b in range(2):
                m = head_mask[b]
                w = probs[2 * p + b, rows]
                wf = w.astype(f32)
                dp = mm_nt(c2 * m, v2)
                delta = jnp.sum(wf * dp, -1, keepdims=True)
                ds = (wf * (dp - delta)).astype(bf16)
                a = mm(ds, k2 * m)
                bb = mm((q2 * m).T, ds)
                c = mm((c2 * m).T, w)
                dq = a if dq is None else dq + a
                dkt = bb if dkt is None else dkt + bb
                dvt = c if dvt is None else dvt + c
            parts.append((dq * scale).astype(bf16))
        dq = jnp.concatenate(parts, axis=0)
        dk = dkt.astype(bf16).T
        dv = dvt.astype(bf16).T
        qkv[:, qa] = dq
        qkv[:, ka] = dk
        qkv[:, va] = dv
        vd[pl.ds(8 * S_BQ, 8), qa] = jnp.sum(dq.astype(f32).reshape(M // 8, 8, 128), axis=0)
        vd[pl.ds(8 * S_BV, 8), qa] = jnp.sum(dv.astype(f32).reshape(M // 8, 8, 128), axis=0)

        @pl.when(i == pairs // 2 - 1)
        def _():
            for copy in qkv_copies:
                copy.start()

        @pl.when(lax.rem(i, 2) == 1)
        def _():
            tick(1 + lax.div(i, 2))

    loop(pairs, attend_back)
    tok_copy.wait_recv()
    for copy in qkv_copies:
        copy.wait_recv()

    for j in range(3):
        g = g_out + 1 + j
        grad_group(
            g,
            X_TOK,
            qkv,
            pl.ds(al(h * DH + j * D, 128), DH),
            qkv_peer,
            pl.ds(j * DH, DH),
        )
        start1(g, (1 + j) % 2)

    sums = jnp.sum(vd[...].reshape(16, 8, D), axis=1)
    fsums = jnp.sum(vf[...].reshape(2, 8, F), axis=1)
    fold = sums[S_ZA : S_ZF + 1, :DH] + sums[S_ZA : S_ZF + 1, DH:]
    for c in range(2):
        pack[c, 0:16, :] = sums[:, c * DH : (c + 1) * DH]
        pack[c, S_ZA : S_ZF + 1, :] = fold
        for j in range(fgroups):
            pack[c, 16 + 2 * j : 18 + 2 * j, :] = fsums[:, c * FH + j * DH : c * FH + (j + 1) * DH]
    pack_copy = to_peer(8, pack.at[oh], packr)

    def input_tile(at):
        acc[:, at] = dres[:, at] + mm_nt(qkv[...], wqkv[at, :])

    tiles(D, input_tile)
    in_near = pltpu.make_async_copy(acc.at[:, cols], input_grad_h.at[mine], lsem.at[11])
    in_near.start()
    in_far = far_copy(acc.at[:, ocols], input_grad_h.at[mine], xs.at[12], xr.at[12], peer)
    in_far.start()

    pack_copy.wait_recv()
    packs[0] = pack[h] + packr[...]
    plane = []
    if use_rs:
        for k, (cx, cy) in enumerate(((1 - x, y), (x, 1 - y), (1 - x, 1 - y))):
            copy = far_copy(packs.at[0], packs.at[1 + k], xs.at[13 + k], xr.at[13 + k], chip(cx, cy, z))
            copy.start()
            plane.append(copy)
    tick(4)

    in_near.wait()
    in_far.wait_send()
    mixed_copy.wait_send()
    mixed[...] = (ctx[...].astype(f32) * par(PHHEAD)).astype(bf16)
    project_out(1.0)
    first_norm(PHH)
    act_copy.wait_send()
    tick(5)
    zsum = []
    if use_rs:
        for copy in plane:
            copy.wait_recv()
        packs[4] = (packs[0] + packs[1]) + (packs[2] + packs[3])
        for d in range(1, zc):
            to = lax.rem(z + d, zc)
            copy = far_copy(
                packs.at[4], packs.at[4 + d], xs.at[17 + d], xr.at[17 + d], chip(x, y, to)
            )
            copy.start()
            zsum.append(copy)
    up(2, False)
    tick(6)
    down()

    def hard_norm(at):
        xh1, inv1 = normed(resid[at, :])
        hidden = (xh1 * par(PG1) + par(PS1)) * par(PHH)
        xh, inv = normed(hidden + acc[at, :] + par(PB_D))
        fin = (xh * par(PG2) + par(PS2)) * par(PHH)
        outb[at, :] = fin.astype(bf16)
        diff = fin - tea[at, :].astype(f32)
        err = jnp.sum(diff * diff, -1, keepdims=True) / D
        keep_ref[at, :] = jnp.broadcast_to(err, (RT, 128))

    row_loop(hard_norm)
    hard_near = pltpu.make_async_copy(outb.at[:, cols], hard_out_h.at[mine], lsem.at[12])
    hard_near.start()
    hard_far = far_copy(outb.at[:, ocols], hard_out_h.at[mine], xs.at[16], xr.at[16], peer)
    hard_far.start()
    pack_copy.wait_send()
    recv_err = vf.at[pl.ds(0, 8), pl.ds(0, M)]
    send_err = vf.at[pl.ds(8, 8), pl.ds(0, M)]
    send_err[...] = errs[...].T[0:8, :]
    err_copy = far_copy(send_err, recv_err, xs.at[17], xr.at[17], peer)
    err_copy.start()

    if use_rs:
        attn_grad_out, up_grad_out, down_grad_out = outs[5:]
        pr = D // n
        grads = []
        for g in range(groups):
            at = acc.at[pl.ds((g // 2) * pr, pr), pl.ds((g % 2) * DH, DH)]
            at[...] = final(g)
            if g < fgroups:
                to = down_grad_out.at[:, pl.ds(g * DH, DH)]
            elif g < 2 * fgroups:
                to = up_grad_out.at[:, pl.ds((g - fgroups) * DH, DH)]
            else:
                to = attn_grad_out.at[g - 2 * fgroups]
            copy = pltpu.make_async_copy(at, to, lsem.at[13 + g])
            copy.start()
            grads.append(copy)
        for copy in zsum:
            copy.wait_recv()
        total = packs[4]
        for d in range(1, zc):
            total = total + packs[4 + d]
        vec_out[...] = total
    else:
        vec_out[...] = packs[0]
        grads_near = pltpu.make_async_copy(G, outs[5], lsem.at[13])
        grads_near.start()
        grads_near.wait()
    err_copy.wait_recv()
    err_out[pl.ds(h, 1), :] = send_err[0:1, :]
    err_out[pl.ds(oh, 1), :] = recv_err[0:1, :]

    hard_near.wait()
    hard_far.wait()
    in_far.wait_recv()
    out_far.wait_recv()
    err_copy.wait_send()
    for copy in remote:
        copy.wait_send()
    tok_copy.wait_send()
    hid_copy.wait_send()
    dbr_copy.wait_send()
    dup_copy.wait_send()
    for copy in qkv_copies:
        copy.wait_send()
    if use_rs:
        for copy in grads:
            copy.wait()
        for copy in plane + zsum:
            copy.wait_send()
        for g in range(groups):
            send1(g, g % 2).wait_send()
            send2(g, g % 2).wait_send()
            for d in range(1, zc):
                send3(g, d).wait_send()


def shards(rows, *args):
    (
        tokens,
        teacher,
        segment_ids,
        valid_rows,
        w_query,
        b_query,
        w_key,
        w_value,
        b_value,
        w_out,
        b_out,
        attention_norm_gain,
        first_shift,
        w_up,
        b_up,
        w_down,
        b_down,
        feedforward_norm_gain,
        second_shift,
        head_alpha,
        head_noise,
        unit_alpha,
        unit_noise,
        hidden_alpha,
        hidden_noise,
        layer_alpha,
        layer_noise,
        hard_heads,
        hard_units,
        hard_hidden,
    ) = args
    DH = tokens.shape[1]
    D = w_query.shape[0]
    FH = w_up.shape[1]
    F = 2 * FH
    blocks, M = segment_ids.shape
    n = rows
    use_rs = n % 4 == 0 and D % n == 0 and (D // n) % 16 == 0
    z_head = gate_value(head_alpha, head_noise)
    z_unit = gate_value(unit_alpha, unit_noise)
    z_hidden = gate_value(hidden_alpha, hidden_noise)
    z_layer = gate_value(layer_alpha, layer_noise)
    wide = lambda v: jnp.broadcast_to(v[:, None], (v.shape[0], HEAD)).reshape(DH)
    pd = jnp.stack(
        [
            v.astype(f32)
            for v in (
                b_query,
                b_value,
                b_out,
                attention_norm_gain,
                first_shift,
                b_down,
                feedforward_norm_gain,
                second_shift,
                z_hidden,
                hard_hidden,
                wide(z_head),
                wide(hard_heads),
                jnp.broadcast_to(z_layer[0], (DH,)),
                jnp.broadcast_to(z_layer[1], (DH,)),
                jnp.zeros((DH,)),
                jnp.zeros((DH,)),
            )
        ]
    )
    zero = jnp.zeros((FH,), f32)
    pf = jnp.stack([b_up.astype(f32), z_unit, hard_units.astype(f32), zero, zero, zero, zero, zero])
    groups = 4 + 2 * (FH // DH)
    fgroups = FH // DH
    zc = n // 4
    pr = D // n
    hbm = pl.BlockSpec(memory_space=pl.ANY)
    vmem = pl.BlockSpec(memory_space=pltpu.VMEM)
    shape = jax.ShapeDtypeStruct
    out_shape = [
        shape(tokens.shape, bf16),
        shape(tokens.shape, f32),
        shape(tokens.shape, bf16),
        shape((2, M), f32),
        shape((24, DH), f32),
    ]
    out_specs = [hbm, hbm, hbm, vmem, vmem]
    if use_rs:
        out_shape += [shape((4, pr, DH), f32), shape((pr, FH), f32), shape((pr, FH), f32)]
        out_specs += [hbm] * 3
        gshape = (groups, zc, 2, 2, pr, DH)
        r1, r2, r3 = (groups, zc, 2, pr, DH), (groups, zc, pr, DH), (groups, zc - 1, pr, DH)
    else:
        out_shape += [shape((groups, D, DH), bf16)]
        out_specs += [hbm]
        gshape = (groups, D, DH)
        r1 = r2 = r3 = (1, 16, 128)
    dma = pltpu.SemaphoreType.DMA
    V = pltpu.VMEM
    scratch = [
        V((M, D), bf16),
        V((M, D), bf16),
        V((D, 3 * D), bf16),
        V((D, D), bf16),
        V((D, F), bf16),
        V((F, D), bf16),
        V((16, D), f32),
        V((8, F), f32),
        V((M, 3 * D), bf16),
        V((M, 3 * DH), bf16),
        V((M, M), bf16),
        V((D // HEAD, M, M), bf16),
        V((M, D), bf16),
        V((M, D), bf16),
        V((M, DH), bf16),
        V((M, D), f32),
        V((M, D), bf16),
        V((M, D), f32),
        V((M, F), bf16),
        V((M, FH), bf16),
        V((M, F), bf16),
        V((M, FH), bf16),
        V((M, D), f32),
        V((M, D), bf16),
        V((3, D, 2 * M), bf16),
        V((16 * 8, D), f32),
        V((16, F), f32),
        V((2, 24, DH), f32),
        V((24, DH), f32),
        V((4 + zc, 24, DH), f32),
        V((M, 128), f32),
        V(gshape, bf16),
        V(r1, bf16),
        V(r2, bf16),
        V(r3, bf16),
        dma((13 + groups,)),
        dma((10,)),
        dma((10,)),
        dma((18 + zc,)),
        dma((18 + zc,)),
        dma((groups,)),
        dma((groups,)),
        dma((groups,)),
        dma((groups,)),
        dma((groups, zc - 1)),
        dma((groups, zc - 1)),
        pltpu.SemaphoreType.REGULAR,
    ]
    results = pl.pallas_call(
        functools.partial(layer_kernel, (n, D, F, M, use_rs)),
        out_shape=out_shape,
        in_specs=[hbm, hbm, vmem, vmem] + [hbm] * 8,
        out_specs=out_specs,
        scratch_shapes=scratch,
        compiler_params=pltpu.CompilerParams(
            collective_id=0, has_side_effects=True, vmem_limit_bytes=VMEM_LIMIT
        ),
    )(
        tokens,
        teacher,
        segment_ids,
        valid_rows,
        w_query,
        w_key,
        w_value,
        w_out,
        w_up,
        w_down,
        pd,
        pf,
    )
    layer_out, input_grad, hard_out, err, vec = results[:5]
    if use_rs:
        attn, up, down = results[5:]
        wq_grad, wk_grad, wv_grad = attn[1], attn[2], attn[3]
        wout_grad = attn[0].T
        down_grad = down.T
    else:
        scatter = lambda v, dim: lax.psum_scatter(
            v.astype(f32), "rows", scatter_dimension=dim, tiled=True
        )
        grads = results[5]
        side = lambda a: a.transpose(1, 0, 2).reshape(D, FH)
        down_grad = scatter(side(grads[:fgroups]).T, 1)
        up = scatter(side(grads[fgroups : 2 * fgroups]), 0)
        wout_grad = scatter(grads[2 * fgroups].T, 1)
        wq_grad, wk_grad, wv_grad = (scatter(grads[2 * fgroups + 1 + j], 0) for j in range(3))
        vec = lax.psum(vec, "rows")
    ff = vec[16:].reshape(fgroups, 2, DH)
    b_up_grad = ff[:, 0].reshape(FH)
    unit_grad = ff[:, 1].reshape(FH) * (1.0 - z_unit) / temper
    hidden_grad = vec[S_ZH] * (z_hidden * (1.0 - z_hidden) / temper)
    head_grad = jnp.sum(vec[S_ZHEAD].reshape(-1, HEAD), -1) * (z_head * (1.0 - z_head) / temper)
    layer_sum = jnp.sum(vec[S_ZA : S_ZF + 1], -1)
    layer_grad = layer_sum * jnp.stack([1.0, z_layer[1]]) * (1.0 - z_layer) / temper
    return (
        layer_out,
        input_grad,
        wq_grad,
        vec[S_BQ],
        wk_grad,
        wv_grad,
        vec[S_BV],
        wout_grad,
        vec[S_BO],
        vec[S_G1],
        vec[S_S1],
        up,
        b_up_grad,
        down_grad,
        vec[S_BD],
        vec[S_G2],
        vec[S_S2],
        head_grad,
        unit_grad,
        hidden_grad,
        layer_grad,
        hard_out,
        err.reshape(-1),
    )


VMEM_LIMIT = 64 * 1024 * 1024 - 256 * 1024


def solution(mesh):
    in_specs = (
        P("rows", "hid"),
        P("rows", "hid"),
        P("rows", None),
        P("rows", None),
        P(None, "hid"),
        P("hid"),
        P(None, "hid"),
        P(None, "hid"),
        P("hid"),
        P("hid", None),
        P("hid"),
        P("hid"),
        P("hid"),
        P(None, "hid"),
        P("hid"),
        P("hid", None),
        P("hid"),
        P("hid"),
        P("hid"),
        P("hid"),
        P("hid"),
        P("hid"),
        P("hid"),
        P("hid"),
        P("hid"),
        P(),
        P(),
        P("hid"),
        P("hid"),
        P("hid"),
    )
    out_specs = (
        P("rows", "hid"),
        P("rows", "hid"),
        P("rows", "hid"),
        P("hid"),
        P("rows", "hid"),
        P("rows", "hid"),
        P("hid"),
        P("hid", "rows"),
        P("hid"),
        P("hid"),
        P("hid"),
        P("rows", "hid"),
        P("hid"),
        P("hid", "rows"),
        P("hid"),
        P("hid"),
        P("hid"),
        P("hid"),
        P("hid"),
        P("hid"),
        P(),
        P("rows", "hid"),
        P("rows"),
    )
    return jax.shard_map(
        functools.partial(shards, mesh.shape["rows"]), mesh=mesh, in_specs=in_specs, out_specs=out_specs, check_vma=False)
```

time: 1180 us -> 166 us (0.14); the launches traced: 1160 us -> 165 us
  waiting for transfers between devices: 754 us -> 0 us
  Pallas kernels: 0 us -> 134 us
  blocking collectives: 129 us -> 0 us
  matrix products: 117 us -> 0 us
  local copies, waits for them, and re-layouts: 93.7 us -> 22 us
  other arithmetic: 51.5 us -> 8.89 us
  between operations: 15.6 us -> 0.75 us
    unnamed x24 -> x0, waiting for transfers between devices: 395 us -> none
    reduce_scatter x5 -> x0, waiting for transfers between devices: 305 us -> none  [the longest x1 142 us: shards(): lax.psum_scatter(w_up_part, 'rows', scatter_dimension=0, tiled=True)]
    pallas_call x0 -> x1, Pallas kernels: none -> 134 us  [shards(): pl.pallas_call(functools.partial(layer_kernel, (n, D, F, M, use_rs)), out...]
    psum x6 -> x0, blocking collectives: 129 us -> none  [the longest x1 76.2 us: shards(): lax.psum((b_query_grad, b_value_grad, b_out_grad, first_gain_grad, first_...]
    dot_general x34 -> x0, matrix products: 117 us -> none  [the longest x8 38.1 us: product(): return jnp.dot(left, right, preferred_element_type=jnp.float32)]
    all_gather x5 -> x0, waiting for transfers between devices: 53.9 us -> none  [the longest x2 21.7 us: layer_pass(): lax.all_gather(hidden_state.astype(jnp.bfloat16), 'hid', axis=1, tiled=True)]
    dynamic_update_slice x4 -> x0, local copies, waits for them, and re-layouts: 31.6 us -> none  [attention_forward(): return lax.map(one_block, (query, keyed, value, segment_ids, valid_rows))]
    reduce_sum x13 -> x2, other arithmetic: 31.6 us -> 1.06 us  [the longest x1 0.94 us: shards(): layer_sum = jnp.sum(vec[S_ZA:S_ZF + 1], -1)]
  transfers between devices with their start and end apart: 17 -> 0, of which waited for: 15 -> 0; matrix products, arithmetic and copies ran while one was open for 4% -> 0% of each run, Pallas kernels for 0% -> 0%
where the time goes in v1:
time: 166 us; the launch traced here: 165 us
  Pallas kernels  134 us (81%)
  local copies, waits for them, and re-layouts  22 us (13%)
  other arithmetic  8.89 us (5%)
    pallas_call x1, Pallas kernels, shards(): pl.pallas_call(functools.partial(layer_kernel, (n, D, F, M, use_rs)), out...  134 us
    another operation x15, local copies, waits for them, and re-layouts, shards(): jnp.stack([v.astype(f32) for v in (b_query, b_value, b_out, attention_nor...  8.08 us
    unnamed x14, local copies, waits for them, and re-layouts  6.88 us

profile of v1, /device:TPU:0, one launch (start us, length us, event | category | flops | bytes accessed | tf_op | source)
XLA Modules:
  0.0 165.3 jit_solution(9225709141799342008)
XLA Ops:
  0.7 0.7 add_divide_fusion.3
  1.3 0.7 add_divide_fusion.2
  2.0 0.7 convert_element_type.30
  3.3 0.6 stack_broadcast_in_dim.10
  3.9 0.6 stack_broadcast_in_dim.9
  4.6 0.7 reshape.68
  5.3 0.7 reshape.69
  6.0 0.7 reshape.70
  6.7 0.7 reshape.71
  7.3 0.7 reshape.72
  8.0 0.7 reshape.73
  8.7 0.7 reshape.74
  9.4 0.7 reshape.75
  10.1 0.7 add_divide_fusion.1
  10.8 0.7 convert_element_type.29
  11.8 1.2 stack.101.refs_10_
  13.0 0.7 reshape.76
  13.7 0.7 add_divide_fusion
  14.5 0.7 convert_element_type.32
  15.2 0.7 stack.107.refs_11_
  15.9 133.8 %shard_map.461 = (bf16[1024,384]{1,0:T(8,128)(2,1)}, f32[1024,384]{1,0:T(8,128)}, bf16[1024,384]{1,0:T(8,128)(2,1)}, f32[2,512]{1,0:T(2,128)}, f32[24,384]{1,0:T...) custom-call(bf16[1024,384]{1,0:T(8,128)(2,1)} %refs_0_.1, bf16[1024,384]{1,0:T(8,128)(2,1)} %refs_1_.1, ...), custom_call_target="tpu_custom_call" | custom-call | tf_op jit(solution)/shard_map/pallas_call | solution.py:904
  149.6 0.9 slice_reduce_fusion.2
  150.6 1.2 fusion.5
  151.8 1.3 copy.53
  153.1 0.7 slice.72
  153.8 1.6 slice_reduce_fusion.3
  158.0 1.7 %slice_bitcast_fusion = (f32[384,48]{0,1:T(8,128)}, f32[48,384]{1,0:T(8,128)}, f32[48,384]{1,0:T(8,128)}, f32[48,384]{1,0:T(8,128)}) fusion(f32[4,48,384]{2,1,0:T(8,128)} %get-tuple-element.33), kind=kLoop, calls=%fused_computation | loop fusion | bytes 589824 | tf_op jit(solution)/shard_map/transpose | solution.py:931
  159.7 2.2 %copy.59 = bf16[1024,384]{1,0:T(8,128)(2,1)} copy(bf16[1024,384]{1,0:T(8,128)(2,1)} %get-tuple-element.80) | data formatting | bytes 1572864
  161.9 1.1 copy.60
  163.0 0.7 copy.61
  163.7 0.7 copy.62
  164.5 0.9 copy.63
  (29 shorter events, 3.5 us)
Async XLA Ops:
  149.6 12.3 %copy-start = (f32[1024,384]{1,0:T(8,128)S(1)}, f32[1024,384]{1,0:T(8,128)}, u32[]{:S(2)}) copy-start(f32[1024,384]{1,0:T(8,128)} %get-tuple-element.81) | copy-start | bytes 4718596
  159.7 3.3 %copy-start.3 = (f32[48,1536]{1,0:T(8,128)S(1)}, f32[48,1536]{1,0:T(8,128)}, u32[]{:S(2)}) copy-start(f32[48,1536]{1,0:T(8,128)} %get-tuple-element.91) | copy-start | bytes 884740
  159.7 4.0 %copy-start.2 = (f32[48,1536]{1,0:T(8,128)S(1)}, f32[48,1536]{1,0:T(8,128)}, u32[]{:S(2)}) copy-start(f32[48,1536]{1,0:T(8,128)} %get-tuple-element.36) | copy-start | bytes 884740
  161.9 2.6 %copy-start.1 = (bf16[1024,384]{1,0:T(8,128)(2,1)S(1)}, bf16[1024,384]{1,0:T(8,128)(2,1)}, u32[]{:S(2)}) copy-start(bf16[1024,384]{1,0:T(8,128)(2,1)} %get-tuple-element.101) | copy-start | bytes 2359300

commit v2 on v1

v2 whole, which is shorter than its diff:
```python
import functools

import jax
import jax.numpy as jnp
from jax import lax
from jax.experimental import pallas as pl
from jax.experimental.pallas import tpu as pltpu
from jax.sharding import PartitionSpec as P

HEAD = 64
f32 = jnp.float32
bf16 = jnp.bfloat16
MESH = pl.DeviceIdType.MESH

temper = 2.0 / 3.0
norm_eps = 1e-12
masked_score = -1e30

PB_Q, PB_K, PB_V, PB_O, PG1, PS1, PB_D, PG2, PS2, PZH, PHH, PZHEAD, PHHEAD, PZA, PZF = range(15)
PGZ1, PSZ1, PGZ2, PSZ2, PHG1, PHS1, PHG2, PHS2 = range(16, 24)
S_BQ, S_BV, S_BO, S_G1, S_S1, S_BD, S_G2, S_S2, S_ZH, S_ZHEAD, S_ZA, S_ZF = range(12)
X_TOK, X_HID, X_DDOWN = range(3)
X_DBR = X_DDOWN


def gate_value(alpha, noise):
    return jax.nn.sigmoid((jnp.log(noise) - jnp.log(1.0 - noise) + alpha) / temper)


def mm(a, b):
    return lax.dot_general(a, b, (((1,), (0,)), ((), ())), preferred_element_type=f32)


def mm_nt(a, b):
    return lax.dot_general(a, b, (((1,), (1,)), ((), ())), preferred_element_type=f32)


def loop(count, body):
    def step(i, carry):
        body(i)
        return carry

    lax.fori_loop(0, count, step, 0)


def al(x, m):
    return pl.multiple_of(x, m)


def params(small, pd, pf, cols, fcols):
    (b_query, b_value, b_out, gain1, shift1, b_down, gain2, shift2) = small[:8]
    hidden_alpha, hidden_noise, hard_hidden = small[8:11]
    b_up, unit_alpha, unit_noise, hard_units = small[11:15]
    head_alpha, head_noise, hard_heads = small[15:18]
    layer_alpha, layer_noise = small[18:20]
    DH = b_query.shape[0]
    FH = b_up.shape[0]

    def row(ref):
        return ref[...].astype(f32).reshape(1, ref.shape[0])

    for k, ref in (
        (PB_Q, b_query),
        (PB_V, b_value),
        (PB_O, b_out),
        (PG1, gain1),
        (PS1, shift1),
        (PB_D, b_down),
        (PG2, gain2),
        (PS2, shift2),
        (PHH, hard_hidden),
    ):
        pd[pl.ds(k, 1), cols] = row(ref)
    pd[pl.ds(PB_K, 1), cols] = jnp.zeros((1, DH), f32)
    pd[pl.ds(PZH, 1), cols] = gate_value(row(hidden_alpha), row(hidden_noise))
    for mask, start in ((PZH, PGZ1), (PHH, PHG1)):
        for k, source in enumerate((PG1, PS1, PG2, PS2)):
            pd[pl.ds(start + k, 1), cols] = pd[pl.ds(source, 1), cols] * pd[pl.ds(mask, 1), cols]
    lane = lax.div(lax.broadcasted_iota(jnp.int32, (1, DH), 1), HEAD)

    def spread(ref):
        wide = jnp.zeros((1, DH), f32)
        for j in range(DH // HEAD):
            wide = jnp.where(lane == j, ref[j].astype(f32), wide)
        return wide

    pd[pl.ds(PZHEAD, 1), cols] = gate_value(spread(head_alpha), spread(head_noise))
    pd[pl.ds(PHHEAD, 1), cols] = spread(hard_heads)
    for k in range(2):
        wide = [jnp.full((1, DH), ref[k], f32) for ref in (layer_alpha, layer_noise)]
        pd[pl.ds(PZA + k, 1), cols] = gate_value(*wide)
    pf[pl.ds(0, 1), fcols] = row(b_up)
    pf[pl.ds(1, 1), fcols] = gate_value(row(unit_alpha), row(unit_noise))
    pf[pl.ds(2, 1), fcols] = row(hard_units)


def layer_kernel(dims, *refs):
    n, D, F, M, use_rs = dims
    DH, FH = D // 2, F // 2
    heads = D // HEAD
    pairs = heads // 2
    groups = 4 + 2 * (FH // DH)
    fgroups = FH // DH
    (
        tok_h,
        tea_h,
        seg_ref,
        valid_ref,
        wq_h,
        wk_h,
        wv_h,
        wout_h,
        wup_h,
        wdown_h,
    ) = refs[:10]
    small = refs[10:30]
    outs = refs[30:36]
    layer_out_h, input_grad_h, hard_out_h, err_out, vec_out, grads_out = outs
    (
        tok,
        tea,
        wqkv,
        wout,
        wup,
        wdown,
        pd,
        pf,
        qkv,
        qkv_peer,
        bias,
        probs,
        ctx,
        mixed,
        mixed_peer,
        resid,
        hbf,
        acc,
        act,
        act_peer,
        gp,
        dup_peer,
        dres,
        dbf,
        xt,
        vd,
        vf,
        pack,
        packr,
        packs,
        errs,
        G,
        recv1,
        recv2,
        recv3,
        lsem,
        ssem,
        rsem,
        xs,
        xr,
        s1,
        r1,
        s2,
        r2,
        s3,
        r3,
        credit,
    ) = refs[36:]

    r = lax.axis_index("rows")
    h = lax.axis_index("hid")
    oh = 1 - h
    peer = (r, oh)
    x = lax.rem(r, 2)
    y = lax.rem(lax.div(r, 2), 2)
    z = lax.div(r, 4)
    zc = n // 4

    def chip(cx, cy, cz):
        return (cz * 4 + cy * 2 + cx, h)

    barrier = pltpu.get_barrier_semaphore()
    partners = [peer]
    if use_rs:
        partners += [chip(1 - x, y, z), chip(x, 1 - y, z), chip(1 - x, 1 - y, z)]
        partners += [chip(x, y, lax.rem(z + d, zc)) for d in range(1, zc)]
    for p in partners:
        pl.semaphore_signal(barrier, inc=1, device_id=p, device_id_type=MESH)
    pl.semaphore_wait(barrier, len(partners))

    cols = pl.ds(al(h * DH, 128), DH)
    ocols = pl.ds(al(oh * DH, 128), DH)
    fcols = pl.ds(al(h * FH, 128), FH)
    ofcols = pl.ds(al(oh * FH, 128), FH)
    mine = pl.ds(al(h * M, 128), M)
    other = pl.ds(al(oh * M, 128), M)
    feeds = [
        (tok_h.at[mine], tok_h.at[other], tok.at[:, cols]),
        (wq_h, wq_h, wqkv.at[:, pl.ds(al(h * DH, 128), DH)]),
        (wk_h, wk_h, wqkv.at[:, pl.ds(al(h * DH + D, 128), DH)]),
        (wv_h, wv_h, wqkv.at[:, pl.ds(al(h * DH + 2 * D, 128), DH)]),
        (wout_h, wout_h, wout.at[cols]),
        (wup_h, wup_h, wup.at[:, fcols]),
        (wdown_h, wdown_h, wdown.at[fcols]),
        (tea_h.at[mine], tea_h.at[other], tea.at[:, cols]),
    ]
    local = []
    remote = []

    def feed(i):
        src, src_other, dst = feeds[i]
        far = pltpu.make_async_remote_copy(
            src_ref=src_other,
            dst_ref=dst,
            send_sem=ssem.at[i],
            recv_sem=rsem.at[i],
            device_id=peer,
            device_id_type=MESH,
        )
        far.start()
        near = pltpu.make_async_copy(src, dst, lsem.at[i])
        near.start()
        local.append(near)
        remote.append(far)

    for i in range(4):
        feed(i)
    params(small, pd, pf, cols, fcols)
    shared = []
    for i, at in ((8, pd.at[:, cols]), (9, pf.at[:, fcols])):
        far = pltpu.make_async_remote_copy(
            src_ref=at,
            dst_ref=at,
            send_sem=ssem.at[i],
            recv_sem=rsem.at[i],
            device_id=peer,
            device_id_type=MESH,
        )
        far.start()
        shared.append(far)
    for i in range(4, 8):
        feed(i)
    remote += shared

    def fed(*which):
        for i in which:
            if i < 8:
                local[i].wait()
            remote[i].wait_recv()

    def to_peer(k, src, dst):
        copy = pltpu.make_async_remote_copy(
            src_ref=src,
            dst_ref=dst,
            send_sem=xs.at[k],
            recv_sem=xr.at[k],
            device_id=peer,
            device_id_type=MESH,
        )
        copy.start()
        return copy

    def far_copy(src, dst, send, recv, device):
        return pltpu.make_async_remote_copy(
            src_ref=src,
            dst_ref=dst,
            send_sem=send,
            recv_sem=recv,
            device_id=device,
            device_id_type=MESH,
        )

    half = zc // 2

    def send1(g, b):
        if b == 0:
            src, to = G.at[g, pl.ds(0, half), :, 1 - x], chip(1 - x, y, z)
        else:
            src, to = G.at[g, pl.ds(half, half), 1 - y], chip(x, 1 - y, z)
        return far_copy(src, recv1.at[g, b], s1.at[g, b], r1.at[g, b], to)

    def send2(g, b):
        zs = pl.ds(b * half, half)
        if b == 0:
            src, to = G.at[g, zs, 1 - y, x], chip(x, 1 - y, z)
        else:
            src, to = G.at[g, zs, y, 1 - x], chip(1 - x, y, z)
        return far_copy(src, recv2.at[g, zs], s2.at[g, b], r2.at[g, b], to)

    def send3(g, d):
        to = lax.rem(z + d, zc)
        return far_copy(
            G.at[g, to, y, x], recv3.at[g, d - 1], s3.at[g, d - 1], r3.at[g, d - 1], chip(x, y, to)
        )

    def stage1(g):
        for b in range(2):
            send1(g, b).wait_recv()

            def body(k, b=b):
                for j in range(2):
                    at = G.at[g, k, j, x] if b == 0 else G.at[g, half + k, y, j]
                    at[...] = (at[...].astype(f32) + recv1[g, b, k, j].astype(f32)).astype(bf16)

            loop(half, body)
            send2(g, b).start()

    def stage2(g):
        for b in range(2):
            send2(g, b).wait_recv()

        def body(k):
            at = G.at[g, k, y, x]
            at[...] = (at[...].astype(f32) + recv2[g, k].astype(f32)).astype(bf16)

        loop(zc, body)
        for d in range(1, zc):
            send3(g, d).start()

    def final(g):
        for d in range(1, zc):
            send3(g, d).wait_recv()
        total = G[g, z, y, x].astype(f32)
        for d in range(1, zc):
            total = total + recv3[g, d - 1].astype(f32)
        return total

    def start1(g):
        if use_rs:
            for b in range(2):
                send1(g, b).start()

    ahead = 3

    def tick(i):
        if not use_rs:
            return
        if i < groups:
            stage1(i)
            if i + ahead < groups:
                start1(i + ahead)
        if 1 <= i <= groups:
            stage2(i - 1)

    RT = 128

    def row_loop(body):
        loop(M // RT, lambda i: body(i, pl.ds(al(i * RT, RT), RT)))

    def add_sum(k, value):
        at = vd.at[pl.ds(8 * k, 8)]
        at[...] = at[...] + jnp.sum(value.reshape(RT // 8, 8, D), axis=0)

    def par(k):
        return pd[pl.ds(k, 1), :]

    def normed(resid_tile):
        mean = jnp.sum(resid_tile, -1, keepdims=True) / D
        var = jnp.sum(resid_tile * resid_tile, -1, keepdims=True) / D - mean * mean
        inv = lax.rsqrt(var + norm_eps)
        return (resid_tile - mean) * inv, inv

    dctx = outb = hbf

    def turned(k, sem, i):
        return far_copy(
            xt.at[k, :, pl.ds(al(i * 128, 128), 128)],
            xt.at[k, :, pl.ds(al(M + i * 128, 128), 128)],
            xs.at[32 + 4 * sem + i],
            xr.at[32 + 4 * sem + i],
            peer,
        )

    def turn(value, k, sem, i):
        xt[k, :, pl.ds(al(i * 128, 128), 128)] = value.T
        turned(k, sem, i).start()

    def turned_in(k, sem):
        for i in range(M // 128):
            turned(k, sem, i).wait_recv()

    def turned_out(k, sem):
        for i in range(M // 128):
            turned(k, sem, i).wait_send()

    NT = 256

    def tiles(count, body):
        loop(count // NT, lambda i: body(pl.ds(al(i * NT, NT), NT)))

    def project_out(gate, gain, shift, keep):
        def body(at):
            acc[:, at] = mm(mixed[...], wout[:, at])

        tiles(D, body)

        def body(i, at):
            value = tok[at, :].astype(f32) + acc[at, :] * gate + par(PB_O)
            resid[at, :] = value
            xh, inv = normed(value)
            hidden = (xh * par(gain) + par(shift)).astype(bf16)
            hbf[at, :] = hidden
            if keep:
                turn(hidden, X_HID, 1, i)

        row_loop(body)

    def up(unit_row, keep):
        def body(at):
            u = mm(hbf[...], wup[:, at]) + pf[pl.ds(0, 1), at]
            u2 = u * u
            half = 0.5 * jnp.tanh(u * (0.7978845608 + (0.7978845608 * 0.044715) * u2)) + 0.5
            act[:, at] = (u * half * pf[pl.ds(unit_row, 1), at]).astype(bf16)
            if keep:
                slope = half + u * (2.0 * half * (1.0 - half)) * (
                    0.7978845608 + (3.0 * 0.7978845608 * 0.044715) * u2
                )
                gp[:, at] = slope.astype(bf16)

        tiles(F, body)

    def down():
        def body(at):
            acc[:, at] = mm(act[...], wdown[:, at])

        tiles(D, body)

    row_seg = seg_ref[pl.ds(h, 1), :].astype(f32)
    row_valid = valid_ref[pl.ds(h, 1), :].astype(f32)
    col_seg = jnp.broadcast_to(row_seg, (128, M)).T[:, :1]
    col_valid = jnp.broadcast_to(row_valid, (128, M)).T
    errs[...] = jnp.zeros_like(errs)
    vd[...] = jnp.zeros_like(vd)
    diagonal = lax.broadcasted_iota(jnp.int32, (M, M), 0) == lax.broadcasted_iota(
        jnp.int32, (M, M), 1
    )
    allowed = ((col_seg == row_seg) & (row_valid > 0)) | diagonal
    bias[...] = jnp.where(allowed, 0.0, masked_score).astype(bf16)
    keep_ref = errs
    keep_ref[...] = col_valid

    def project_in(first):
        def body(part):
            at = pl.ds(al(first, 128), DH)
            wide = pl.ds(al(part * D + first, 128), DH)
            value = mm(tok[...], wqkv[:, wide]) + pd[pl.ds(part, 1), at]
            value = value.astype(bf16).astype(f32) * jnp.where(part == 0, HEAD**-0.5, 1.0)
            qkv[:, wide] = value.astype(bf16)

        loop(3, body)

    local[0].wait()
    remote[0].wait_recv()
    for i in (1, 2, 3):
        local[i].wait()
    project_in(h * DH)
    for i in (1, 2, 3, 8, 9):
        remote[i].wait_recv()
    project_in(oh * DH)

    loop(M // 128, lambda i: turn(tok[pl.ds(al(i * 128, 128), 128), :], X_TOK, 0, i))

    lane = lax.broadcasted_iota(jnp.int32, (1, 2 * HEAD), 1)
    head_mask = [(lane < HEAD).astype(bf16), (lane >= HEAD).astype(bf16)]

    QT = 512

    def attend(i):
        p = lax.div(i, M // QT)
        rows = pl.ds(al(lax.rem(i, M // QT) * QT, QT), QT)
        at = pl.ds(al(p * 128, 128), 128)
        q2 = qkv[rows, at]
        k2 = qkv[:, pl.ds(al(p * 128 + D, 128), 128)]
        v2 = qkv[:, pl.ds(al(p * 128 + 2 * D, 128), 128)]
        total = None
        for b in range(2):
            s = mm_nt(q2 * head_mask[b], k2) + bias[rows, :].astype(f32)
            e = jnp.exp(s - jnp.max(s, -1, keepdims=True))
            w = (e * (1.0 / jnp.sum(e, -1, keepdims=True))).astype(bf16)
            probs[2 * p + b, rows] = w
            part = mm(w, v2 * head_mask[b])
            total = part if total is None else total + part
        ctx[rows, at] = total.astype(bf16)
        mixed[rows, at] = (total * pd[pl.ds(PZHEAD, 1), at]).astype(bf16)

    loop(pairs * (M // QT), attend)
    mixed_copy = to_peer(4, mixed.at[:, ocols], mixed_peer)

    fed(4)
    project_out(par(PZA), PGZ1, PSZ1, True)
    fed(5)
    up(1, True)
    act_copy = to_peer(5, act.at[:, ofcols], act_peer)
    fed(6, 7)
    down()

    def second_norm(i, at):
        xh1, inv1 = normed(resid[at, :])
        hidden = xh1 * par(PGZ1) + par(PSZ1)
        dn = acc[at, :]
        xh, inv = normed(hidden + par(PZF) * dn + par(PB_D))
        fin = xh * par(PGZ2) + par(PSZ2)
        outb[at, :] = fin.astype(bf16)
        d = keep_ref[at, :][:, :1] * (fin - tea[at, :].astype(f32))
        add_sum(S_S2, d)
        add_sum(S_G2, d * xh)
        e = d * par(PGZ2)
        dr = inv * (
            e - jnp.sum(e, -1, keepdims=True) / D - xh * (jnp.sum(e * xh, -1, keepdims=True) / D)
        )
        add_sum(S_BD, dr)
        add_sum(S_ZF, dr * dn)
        dres[at, :] = dr
        down_grad_rows = (dr * par(PZF)).astype(bf16)
        dbf[at, :] = down_grad_rows
        turn(down_grad_rows, X_DDOWN, 2, i)

    row_loop(second_norm)
    out_near = pltpu.make_async_copy(outb.at[:, cols], layer_out_h.at[mine], lsem.at[10])
    out_near.start()
    out_far = to_peer(6, outb.at[:, ocols], layer_out_h.at[mine])

    def dactive_tile(at):
        da = mm_nt(dbf[...], wdown[at, :])
        su = jnp.sum((da * act[:, at].astype(f32)).reshape(M // 8, 8, NT), axis=0)
        vf[pl.ds(8, 8), at] = su
        du = (da * pf[pl.ds(1, 1), at] * gp[:, at].astype(f32)).astype(bf16)
        gp[:, at] = du
        vf[pl.ds(0, 8), at] = jnp.sum(du.astype(f32).reshape(M // 8, 8, NT), axis=0)

    early = F // NT // 3
    loop(early, lambda i: dactive_tile(pl.ds(al(i * NT, NT), NT)))

    GT = D // zc if use_rs else D // 4

    def store_grad(g, i, value):
        if use_rs:
            G[g, i] = value.astype(bf16).reshape(2, 2, D // n, DH)
        else:
            G[g, pl.ds(al(i * GT, GT), GT)] = value.astype(bf16)

    def grad_group(g, k, own, far):
        def body(i):
            at = pl.ds(al(i * GT, GT), GT)
            value = mm(xt[k, at, pl.ds(0, M)], own()) + mm(xt[k, at, pl.ds(M, M)], far())
            for b in range(value.shape[1] // DH):
                store_grad(g + b, i, value[:, b * DH : (b + 1) * DH])

        loop(D // GT, body)

    turned_in(X_DDOWN, 2)
    act_copy.wait_recv()

    def down_grad(i):
        grad_group(
            2 * i,
            X_DDOWN,
            lambda: act[:, pl.ds(al(h * FH + i * D, 128), D)],
            lambda: act_peer[:, pl.ds(al(i * D, 128), D)],
        )

    down_grad(0)
    start1(0)
    start1(1)
    down_grad(1)
    start1(2)
    pl.semaphore_signal(credit, inc=1, device_id=peer, device_id_type=MESH)

    loop(F // NT - early, lambda i: dactive_tile(pl.ds(al((i + early) * NT, NT), NT)))
    dup_copy = to_peer(7, gp.at[:, ofcols], dup_peer)

    def dhidden_tile(at):
        acc[:, at] = mm_nt(gp[...], wup[at, :])

    tiles(D, dhidden_tile)
    tick(0)

    turned_in(X_HID, 1)
    dup_copy.wait_recv()

    def up_grad(i):
        grad_group(
            fgroups + 2 * i,
            X_HID,
            lambda: gp[:, pl.ds(al(h * FH + i * D, 128), D)],
            lambda: dup_peer[:, pl.ds(al(i * D, 128), D)],
        )

    loop(fgroups // 2, up_grad)

    out_near.wait()
    out_far.wait_send()
    turned_out(X_DDOWN, 2)
    pl.semaphore_wait(credit, 1)

    def first_norm_back(i, at):
        value = resid[at, :]
        xh, inv = normed(value)
        dh = dres[at, :] + acc[at, :]
        add_sum(S_S1, dh)
        add_sum(S_G1, dh * xh)
        e = dh * par(PGZ1)
        dr = inv * (
            e - jnp.sum(e, -1, keepdims=True) / D - xh * (jnp.sum(e * xh, -1, keepdims=True) / D)
        )
        add_sum(S_BO, dr)
        add_sum(S_ZA, dr * (value - tok[at, :].astype(f32) - par(PB_O)))
        dres[at, :] = dr
        branch_grad = (dr * par(PZA)).astype(bf16)
        dbf[at, :] = branch_grad
        turn(branch_grad, X_DBR, 3, i)

    tick(1)
    row_loop(first_norm_back)
    def dmixed_tile(at):
        dm = mm_nt(dbf[...], wout[at, :])
        vd[pl.ds(8 * S_ZHEAD, 8), at] = jnp.sum(
            (dm * ctx[:, at].astype(f32)).reshape(M // 8, 8, NT), axis=0
        )
        dctx[:, at] = (dm * pd[pl.ds(PZHEAD, 1), at]).astype(bf16)

    tiles(D, dmixed_tile)
    turned_in(X_DBR, 3)
    mixed_copy.wait_recv()
    g_out = 2 * fgroups
    grad_group(g_out, X_DBR, lambda: mixed[:, cols], lambda: mixed_peer[...])
    tick(2)

    own_pairs = pairs // 2

    def send_pair(j, t):
        return far_copy(
            qkv.at[:, pl.ds(al(oh * DH + j * 128 + t * D, 128), 128)],
            qkv_peer.at[:, pl.ds(al(j * DH + t * 128, 128), 128)],
            xs.at[20 + 3 * j + t],
            xr.at[20 + 3 * j + t],
            peer,
        )

    scale = HEAD**-0.5

    def attend_back(i):
        j, own = lax.div(i, 2), lax.rem(i, 2)
        p = lax.rem(oh + own, 2) * own_pairs + j
        qa = pl.ds(al(p * 128, 128), 128)
        ka = pl.ds(al(p * 128 + D, 128), 128)
        va = pl.ds(al(p * 128 + 2 * D, 128), 128)
        k2, v2 = qkv[:, ka], qkv[:, va]
        dkt = dvt = None
        parts = []
        for t in range(M // 256):
            rows = pl.ds(t * 256, 256)
            q2, c2 = qkv[rows, qa], dctx[rows, qa]
            dq = None
            for b in range(2):
                m = head_mask[b]
                w = probs[2 * p + b, rows]
                wf = w.astype(f32)
                dp = mm_nt(c2 * m, v2)
                delta = jnp.sum(wf * dp, -1, keepdims=True)
                ds = (wf * (dp - delta)).astype(bf16)
                a = mm(ds, k2 * m)
                bb = mm((q2 * m).T, ds)
                c = mm((c2 * m).T, w)
                dq = a if dq is None else dq + a
                dkt = bb if dkt is None else dkt + bb
                dvt = c if dvt is None else dvt + c
            parts.append((dq * scale).astype(bf16))
        dq = jnp.concatenate(parts, axis=0)
        dk = dkt.astype(bf16).T
        dv = dvt.astype(bf16).T
        qkv[:, qa] = dq
        qkv[:, ka] = dk
        qkv[:, va] = dv
        vd[pl.ds(8 * S_BQ, 8), qa] = jnp.sum(dq.astype(f32).reshape(M // 8, 8, 128), axis=0)
        vd[pl.ds(8 * S_BV, 8), qa] = jnp.sum(dv.astype(f32).reshape(M // 8, 8, 128), axis=0)

        @pl.when(own == 0)
        def _():
            for t in range(3):
                send_pair(j, t).start()

        @pl.when(own == 1)
        def _():
            for t in range(3):
                send_pair(j, t).wait_recv()
            grad_group(
                g_out + 1 + j,
                X_TOK,
                lambda: jnp.concatenate(
                    [qkv[:, pl.ds(al(h * DH + j * 128 + t * D, 128), 128)] for t in range(3)], axis=1
                ),
                lambda: qkv_peer[:, pl.ds(al(j * DH, 128), DH)],
            )

        for at_step, k in ((2, 3), (5, 4)):

            @pl.when(i == at_step)
            def _(k=k):
                tick(k)

    turned_in(X_TOK, 0)
    loop(pairs, attend_back)

    hidden_sum = 0.0
    for shift_row, gain_row, gain, shift in ((S_S1, S_G1, PG1, PS1), (S_S2, S_G2, PG2, PS2)):
        plain, with_xh = vd[pl.ds(8 * shift_row, 8), :], vd[pl.ds(8 * gain_row, 8), :]
        hidden_sum = hidden_sum + par(gain) * with_xh + par(shift) * plain
        vd[pl.ds(8 * shift_row, 8), :] = plain * par(PZH)
        vd[pl.ds(8 * gain_row, 8), :] = with_xh * par(PZH)
    vd[pl.ds(8 * S_ZH, 8), :] = hidden_sum * (par(PZH) * (1.0 - par(PZH)) / temper)
    zhead, za, zu = par(PZHEAD), pd[pl.ds(PZA, 2), :], pf[pl.ds(1, 1), :]
    for k, factor in (
        (S_ZHEAD, zhead * (1.0 - zhead) / temper),
        (S_ZA, (1.0 - za[0:1]) / temper),
        (S_ZF, za[1:2] * (1.0 - za[1:2]) / temper),
    ):
        vd[pl.ds(8 * k, 8), :] = vd[pl.ds(8 * k, 8), :] * factor
    vf[pl.ds(8, 8), :] = vf[pl.ds(8, 8), :] * ((1.0 - zu) / temper)
    sums = jnp.sum(vd[...].reshape(16, 8, D), axis=1)
    fsums = jnp.sum(vf[...].reshape(2, 8, F), axis=1)
    fold = sums[S_ZA : S_ZF + 1, :DH] + sums[S_ZA : S_ZF + 1, DH:]
    for c in range(2):
        pack[c, 0:16, :] = sums[:, c * DH : (c + 1) * DH]
        pack[c, S_ZA : S_ZF + 1, :] = fold
        for j in range(fgroups):
            pack[c, 16 + 2 * j : 18 + 2 * j, :] = fsums[:, c * FH + j * DH : c * FH + (j + 1) * DH]
    pack_copy = to_peer(8, pack.at[oh], packr)

    def input_tile(at):
        acc[:, at] = dres[:, at] + mm_nt(qkv[...], wqkv[at, :])

    tiles(D, input_tile)
    in_near = pltpu.make_async_copy(acc.at[:, cols], input_grad_h.at[mine], lsem.at[11])
    in_near.start()
    in_far = far_copy(acc.at[:, ocols], input_grad_h.at[mine], xs.at[12], xr.at[12], peer)
    in_far.start()

    pack_copy.wait_recv()
    packs[0] = pack[h] + packr[...]
    plane = []
    if use_rs:
        for k, (cx, cy) in enumerate(((1 - x, y), (x, 1 - y), (1 - x, 1 - y))):
            copy = far_copy(packs.at[0], packs.at[1 + k], xs.at[13 + k], xr.at[13 + k], chip(cx, cy, z))
            copy.start()
            plane.append(copy)
    tick(5)

    in_near.wait()
    in_far.wait_send()
    mixed_copy.wait_send()
    mixed[...] = (ctx[...].astype(f32) * par(PHHEAD)).astype(bf16)
    project_out(1.0, PHG1, PHS1, False)
    act_copy.wait_send()
    tick(6)
    zsum = []
    if use_rs:
        for copy in plane:
            copy.wait_recv()
        packs[4] = (packs[0] + packs[1]) + (packs[2] + packs[3])
        for d in range(1, zc):
            to = lax.rem(z + d, zc)
            copy = far_copy(
                packs.at[4], packs.at[4 + d], xs.at[47 + d], xr.at[47 + d], chip(x, y, to)
            )
            copy.start()
            zsum.append(copy)
    up(2, False)
    tick(7)
    down()
    tick(8)

    def hard_norm(i, at):
        xh1, inv1 = normed(resid[at, :])
        hidden = xh1 * par(PHG1) + par(PHS1)
        xh, inv = normed(hidden + acc[at, :] + par(PB_D))
        fin = xh * par(PHG2) + par(PHS2)
        outb[at, :] = fin.astype(bf16)
        diff = fin - tea[at, :].astype(f32)
        err = jnp.sum(diff * diff, -1, keepdims=True) / D
        keep_ref[at, :] = jnp.broadcast_to(err, (RT, 128))

    row_loop(hard_norm)
    hard_near = pltpu.make_async_copy(outb.at[:, cols], hard_out_h.at[mine], lsem.at[12])
    hard_near.start()
    hard_far = far_copy(outb.at[:, ocols], hard_out_h.at[mine], xs.at[16], xr.at[16], peer)
    hard_far.start()
    pack_copy.wait_send()
    recv_err = vf.at[pl.ds(0, 8), pl.ds(0, M)]
    send_err = vf.at[pl.ds(8, 8), pl.ds(0, M)]
    send_err[...] = errs[...].T[0:8, :]
    err_copy = far_copy(send_err, recv_err, xs.at[17], xr.at[17], peer)
    err_copy.start()

    for i in range(9, groups + 1):
        tick(i)
    if use_rs:
        pr = D // n
        grads = []
        for g in range(groups):
            at = acc.at[pl.ds((g // 2) * pr, pr), pl.ds((g % 2) * DH, DH)]
            at[...] = final(g)
            copy = pltpu.make_async_copy(at, grads_out.at[g], lsem.at[13 + g])
            copy.start()
            grads.append(copy)
        for copy in zsum:
            copy.wait_recv()
        total = packs[4]
        for d in range(1, zc):
            total = total + packs[4 + d]
        vec_out[...] = total
    else:
        vec_out[...] = packs[0]
        grads_near = pltpu.make_async_copy(G, grads_out, lsem.at[13])
        grads_near.start()
        grads_near.wait()
    err_copy.wait_recv()
    err_out[pl.ds(h, 1), :] = send_err[0:1, :]
    err_out[pl.ds(oh, 1), :] = recv_err[0:1, :]

    hard_near.wait()
    hard_far.wait()
    in_far.wait_recv()
    out_far.wait_recv()
    err_copy.wait_send()
    for copy in remote:
        copy.wait_send()
    turned_out(X_TOK, 0)
    turned_out(X_HID, 1)
    turned_out(X_DBR, 3)
    dup_copy.wait_send()
    for j in range(own_pairs):
        for t in range(3):
            send_pair(j, t).wait_send()
    if use_rs:
        for copy in grads:
            copy.wait()
        for copy in plane + zsum:
            copy.wait_send()
        for g in range(groups):
            for b in range(2):
                send1(g, b).wait_send()
                send2(g, b).wait_send()
            for d in range(1, zc):
                send3(g, d).wait_send()


def shards(rows, *args):
    (
        tokens,
        teacher,
        segment_ids,
        valid_rows,
        w_query,
        b_query,
        w_key,
        w_value,
        b_value,
        w_out,
        b_out,
        attention_norm_gain,
        first_shift,
        w_up,
        b_up,
        w_down,
        b_down,
        feedforward_norm_gain,
        second_shift,
        head_alpha,
        head_noise,
        unit_alpha,
        unit_noise,
        hidden_alpha,
        hidden_noise,
        layer_alpha,
        layer_noise,
        hard_heads,
        hard_units,
        hard_hidden,
    ) = args
    DH = tokens.shape[1]
    D = w_query.shape[0]
    FH = w_up.shape[1]
    F = 2 * FH
    blocks, M = segment_ids.shape
    n = rows
    use_rs = n % 8 == 0 and D % n == 0 and (D // n) % 16 == 0
    groups = 4 + 2 * (FH // DH)
    fgroups = FH // DH
    zc = n // 4
    pr = D // n
    hbm = pl.BlockSpec(memory_space=pl.ANY)
    vmem = pl.BlockSpec(memory_space=pltpu.VMEM)
    smem = pl.BlockSpec(memory_space=pltpu.SMEM)
    shape = jax.ShapeDtypeStruct
    out_shape = [
        shape(tokens.shape, bf16),
        shape(tokens.shape, f32),
        shape(tokens.shape, bf16),
        shape((2, M), f32),
        shape((24, DH), f32),
    ]
    out_specs = [hbm, hbm, hbm, vmem, vmem, hbm]
    if use_rs:
        out_shape += [shape((groups, pr, DH), f32)]
        gshape = (groups, zc, 2, 2, pr, DH)
        r1, r2, r3 = (groups, 2, zc // 2, 2, pr, DH), (groups, zc, pr, DH), (groups, zc - 1, pr, DH)
    else:
        out_shape += [shape((groups, D, DH), bf16)]
        gshape = (groups, D, DH)
        r1 = r2 = r3 = (1, 16, 128)
    dma = pltpu.SemaphoreType.DMA
    V = pltpu.VMEM
    scratch = [
        V((M, D), bf16),
        V((M, D), bf16),
        V((D, 3 * D), bf16),
        V((D, D), bf16),
        V((D, F), bf16),
        V((F, D), bf16),
        V((24, D), f32),
        V((8, F), f32),
        V((M, 3 * D), bf16),
        V((M, 3 * DH), bf16),
        V((M, M), bf16),
        V((D // HEAD, M, M), bf16),
        V((M, D), bf16),
        V((M, D), bf16),
        V((M, DH), bf16),
        V((M, D), f32),
        V((M, D), bf16),
        V((M, D), f32),
        V((M, F), bf16),
        V((M, FH), bf16),
        V((M, F), bf16),
        V((M, FH), bf16),
        V((M, D), f32),
        V((M, D), bf16),
        V((3, D, 2 * M), bf16),
        V((16 * 8, D), f32),
        V((16, F), f32),
        V((2, 24, DH), f32),
        V((24, DH), f32),
        V((4 + zc, 24, DH), f32),
        V((M, 128), f32),
        V(gshape, bf16),
        V(r1, bf16),
        V(r2, bf16),
        V(r3, bf16),
        dma((13 + groups,)),
        dma((10,)),
        dma((10,)),
        dma((48 + zc,)),
        dma((48 + zc,)),
        dma((groups, 2)),
        dma((groups, 2)),
        dma((groups, 2)),
        dma((groups, 2)),
        dma((groups, zc - 1)),
        dma((groups, zc - 1)),
        pltpu.SemaphoreType.REGULAR,
    ]
    results = pl.pallas_call(
        functools.partial(layer_kernel, (n, D, F, M, use_rs)),
        out_shape=out_shape,
        in_specs=[hbm, hbm, vmem, vmem] + [hbm] * 6 + [vmem] * 15 + [smem] * 5,
        out_specs=out_specs,
        scratch_shapes=scratch,
        compiler_params=pltpu.CompilerParams(
            collective_id=0, has_side_effects=True, vmem_limit_bytes=VMEM_LIMIT
        ),
    )(
        tokens,
        teacher,
        segment_ids,
        valid_rows,
        w_query,
        w_key,
        w_value,
        w_out,
        w_up,
        w_down,
        b_query,
        b_value,
        b_out,
        attention_norm_gain,
        first_shift,
        b_down,
        feedforward_norm_gain,
        second_shift,
        hidden_alpha,
        hidden_noise,
        hard_hidden,
        b_up,
        unit_alpha,
        unit_noise,
        hard_units,
        head_alpha,
        head_noise,
        hard_heads,
        layer_alpha,
        layer_noise,
    )
    layer_out, input_grad, hard_out, err, vec, grads = results
    if not use_rs:
        vec = lax.psum(vec, "rows")
        side = lambda a: a.transpose(1, 0, 2).reshape(D, -1)
        grads = lax.psum_scatter(
            side(grads).astype(f32), "rows", scatter_dimension=0, tiled=True
        )
        grads = grads.reshape(pr, groups, DH).transpose(1, 0, 2)
    small = (DH,)
    wide = (FH,)
    finished = pl.pallas_call(
        functools.partial(finish_kernel, fgroups),
        out_shape=[
            shape(s, d)
            for s, d in (
                (tokens.shape, bf16),
                (tokens.shape, f32),
                ((pr, DH), f32),
                (small, f32),
                ((pr, DH), f32),
                ((pr, DH), f32),
                (small, f32),
                ((pr, DH), f32),
                (small, f32),
                (small, f32),
                (small, f32),
                ((pr, FH), f32),
                (wide, f32),
                ((pr, FH), f32),
                (small, f32),
                (small, f32),
                (small, f32),
                (head_alpha.shape, f32),
                (wide, f32),
                (small, f32),
                (layer_alpha.shape, f32),
                (tokens.shape, bf16),
                ((tokens.shape[0],), f32),
            )
        ],
        in_specs=[hbm, hbm, hbm] + [vmem] * 3,
        out_specs=[hbm, hbm] + [vmem] * 15 + [smem, vmem, vmem, smem, hbm, vmem],
        scratch_shapes=[V(tokens.shape, bf16), V(tokens.shape, f32), V(tokens.shape, bf16)]
        + [dma((3, 4))] * 2,
    )(layer_out, input_grad, hard_out, err, vec, grads)
    finished = list(finished)
    for k in (7, 13):
        finished[k] = finished[k].T
    return tuple(finished)


def finish_kernel(fgroups, *refs):
    layer_in, input_in, hard_in, err, vec, grads = refs[:6]
    (
        layer_out,
        input_grad,
        wq_grad,
        bq_grad,
        wk_grad,
        wv_grad,
        bv_grad,
        wout_grad,
        bo_grad,
        g1_grad,
        s1_grad,
        wup_grad,
        bup_grad,
        wdown_grad,
        bd_grad,
        g2_grad,
        s2_grad,
        head_grad,
        unit_grad,
        hidden_grad,
        layer_grad,
        hard_out,
        hard_err,
    ) = refs[6:29]
    buffers, (in_sem, out_sem) = refs[29:32], refs[32:34]
    ways = []
    for k, (a, b) in enumerate(
        ((input_in, input_grad), (layer_in, layer_out), (hard_in, hard_out))
    ):
        buffer = buffers[(1, 0, 2)[k]]
        size = a.shape[0] // 4
        for c in range(4):
            at = pl.ds(c * size, size)
            ways.append(
                (
                    pltpu.make_async_copy(a.at[at], buffer.at[at], in_sem.at[k, c]),
                    pltpu.make_async_copy(buffer.at[at], b.at[at], out_sem.at[k, c]),
                )
            )
    for near, _ in ways:
        near.start()
    for near, far in ways:
        near.wait()
        far.start()
    DH = bq_grad.shape[0]
    M = err.shape[1]

    def row(k):
        return vec[pl.ds(k, 1), :]

    for k, ref in (
        (S_BQ, bq_grad),
        (S_BV, bv_grad),
        (S_BO, bo_grad),
        (S_G1, g1_grad),
        (S_S1, s1_grad),
        (S_BD, bd_grad),
        (S_G2, g2_grad),
        (S_S2, s2_grad),
        (S_ZH, hidden_grad),
    ):
        ref[...] = row(k).reshape(DH)
    bup_grad[...] = jnp.concatenate([row(16 + 2 * j) for j in range(fgroups)], axis=1).reshape(
        fgroups * DH
    )
    unit_grad[...] = jnp.concatenate([row(17 + 2 * j) for j in range(fgroups)], axis=1).reshape(
        fgroups * DH
    )
    lane = lax.div(lax.broadcasted_iota(jnp.int32, (1, DH), 1), HEAD)
    heads = row(S_ZHEAD)
    for j in range(DH // HEAD):
        head_grad[j] = jnp.sum(jnp.where(lane == j, heads, 0.0))
    layer_grad[0] = jnp.sum(row(S_ZA))
    layer_grad[1] = jnp.sum(row(S_ZF))
    for b in range(2):
        hard_err[pl.ds(b * M, M)] = err[pl.ds(b, 1), :].reshape(M)
    for g in range(fgroups):
        at = pl.ds(g * DH, DH)
        wdown_grad[:, at] = grads[g]
        wup_grad[:, at] = grads[fgroups + g]
    wout_grad[...] = grads[2 * fgroups]
    for j in range(3):
        to = pl.ds(j * 128, 128)
        for t, ref in enumerate((wq_grad, wk_grad, wv_grad)):
            ref[:, to] = grads[2 * fgroups + 1 + j][:, t * 128 : (t + 1) * 128]
    for _, far in ways:
        far.wait()


VMEM_LIMIT = 64 * 1024 * 1024 - 256 * 1024


def solution(mesh):
    in_specs = (
        P("rows", "hid"),
        P("rows", "hid"),
        P("rows", None),
        P("rows", None),
        P(None, "hid"),
        P("hid"),
        P(None, "hid"),
        P(None, "hid"),
        P("hid"),
        P("hid", None),
        P("hid"),
        P("hid"),
        P("hid"),
        P(None, "hid"),
        P("hid"),
        P("hid", None),
        P("hid"),
        P("hid"),
        P("hid"),
        P("hid"),
        P("hid"),
        P("hid"),
        P("hid"),
        P("hid"),
        P("hid"),
        P(),
        P(),
        P("hid"),
        P("hid"),
        P("hid"),
    )
    out_specs = (
        P("rows", "hid"),
        P("rows", "hid"),
        P("rows", "hid"),
        P("hid"),
        P("rows", "hid"),
        P("rows", "hid"),
        P("hid"),
        P("hid", "rows"),
        P("hid"),
        P("hid"),
        P("hid"),
        P("rows", "hid"),
        P("hid"),
        P("hid", "rows"),
        P("hid"),
        P("hid"),
        P("hid"),
        P("hid"),
        P("hid"),
        P("hid"),
        P(),
        P("rows", "hid"),
        P("rows"),
    )
    return jax.shard_map(
        functools.partial(shards, mesh.shape["rows"]), mesh=mesh, in_specs=in_specs, out_specs=out_specs, check_vma=False)
```

time: 166 us -> 125 us (0.75)
  local copies, waits for them, and re-layouts: 22 us -> 0 us
  Pallas kernels: 134 us -> 123 us
  other arithmetic: 8.89 us -> 0 us
    pallas_call x1, Pallas kernels: 134 us -> 118 us  [shards(): pl.pallas_call(functools.partial(layer_kernel, (n, D, F, M, use_rs)), out...]
    another operation x24 -> x0, local copies, waits for them, and re-layouts: 10.2 us -> none  [the longest x15 8.08 us: shards(): jnp.stack([v.astype(f32) for v in (b_query, b_value, b_out, attention_nor...]
    unnamed x14 -> x0, local copies, waits for them, and re-layouts: 6.88 us -> none
    pallas_call x0 -> x1, Pallas kernels: none -> 5.01 us  [shards(): pl.pallas_call(functools.partial(finish_kernel, fgroups), out_shape=[shap...]
    div x6 -> x0, other arithmetic: 4.66 us -> none  [the longest x4 2.82 us: gate_value(): jax.nn.sigmoid((jnp.log(noise) - jnp.log(1.0 - noise) + alpha) / temper)]
    slice x4 -> x0, local copies, waits for them, and re-layouts: 2.98 us -> none  [the longest x1 1.65 us: shards(): hidden_grad = vec[S_ZH] * (z_hidden * (1.0 - z_hidden) / temper)]
    convert_element_type x3 -> x0, other arithmetic: 2.06 us -> none  [the longest x2 1.36 us: shards(): v.astype(f32)]
    transpose x1 -> x0, local copies, waits for them, and re-layouts: 1.7 us -> none  [shards(): wout_grad = attn[0].T]
where the time goes in v2:
time: 125 us; the launch traced here: 124 us
  Pallas kernels  123 us (98%)
    pallas_call x1, Pallas kernels, shards(): pl.pallas_call(functools.partial(layer_kernel, (n, D, F, M, use_rs)), out...  118 us
    pallas_call x1, Pallas kernels, shards(): pl.pallas_call(functools.partial(finish_kernel, fgroups), out_shape=[shap...  5.01 us

profile of v2, /device:TPU:0, one launch (start us, length us, event | category | flops | bytes accessed | tf_op | source)
XLA Modules:
  0.0 124.3 jit_solution(6064312443736937141)
XLA Ops:
  0.7 118.5 %shard_map.461 = (bf16[1024,384]{1,0:T(8,128)(2,1)}, f32[1024,384]{1,0:T(8,128)}, bf16[1024,384]{1,0:T(8,128)(2,1)}, f32[2,512]{1,0:T(2,128)}, f32[24,384]{1,0:T(8,128)}, /*index=5*/f32[12,48,384]{2,1,0:T(8,128)}) custom-call(bf16[1024,384]{1,0:T(8,128)(2,1)} %refs_0_.1, bf16[1024,384]{1,0:T(8,128)(2,1)} %refs_1_.1, s32[2,512]{1,0:T(2,128)} %refs_2_.1, ...), custom_call_target="tpu_custom_call" | custom-call | tf_op jit(solution)/shard_map/pallas_call | solution.py:962
  119.2 5.0 %shard_map.462 = (bf16[1024,384]{1,0:T(8,128)(2,1)}, f32[1024,384]{1,0:T(8,128)}, f32[48,384]{1,0:T(8,128)}, f32[384]{0:T(512)}, f32[48,384]{1,0:T(8,128)}, /*in...) custom-call(bf16[1024,384]{1,0:T(8,128)(2,1)} %get-tuple-element.52., ...), custom_call_target="tpu_custom_call" | custom-call | tf_op jit(solution)/shard_map/pallas_call | solution.py:1013

commit v3 on v2

--- a/solution.py
+++ b/solution.py
@@ -19,8 +19,8 @@
 PB_Q, PB_K, PB_V, PB_O, PG1, PS1, PB_D, PG2, PS2, PZH, PHH, PZHEAD, PHHEAD, PZA, PZF = range(15)
 PGZ1, PSZ1, PGZ2, PSZ2, PHG1, PHS1, PHG2, PHS2 = range(16, 24)
 S_BQ, S_BV, S_BO, S_G1, S_S1, S_BD, S_G2, S_S2, S_ZH, S_ZHEAD, S_ZA, S_ZF = range(12)
-X_TOK, X_HID, X_DDOWN = range(3)
-X_DBR = X_DDOWN
+X_HID, X_DDOWN = range(2)
+X_TOK, X_DBR = X_HID, X_DDOWN
 
 
 def gate_value(alpha, noise):
@@ -131,7 +131,6 @@
         probs,
         ctx,
         mixed,
-        mixed_peer,
         resid,
         hbf,
         acc,
@@ -163,6 +162,9 @@
         r2,
         s3,
         r3,
+        zr,
+        zs,
+        zw,
         credit,
     ) = refs[36:]
 
@@ -271,75 +273,209 @@
 
     half = zc // 2
 
-    def send1(g, b):
+    last = groups - 1
+    runs = 1
+
+    def place(v):
+        if v < last:
+            return v, pl.ds(0, DH)
+        return last, pl.ds(0, DH)
+
+    def send1(v, b):
+        g, cs = place(v)
         if b == 0:
-            src, to = G.at[g, pl.ds(0, half), :, 1 - x], chip(1 - x, y, z)
+            src, to = G.at[g, pl.ds(0, half), :, 1 - x, :, cs], chip(1 - x, y, z)
         else:
-            src, to = G.at[g, pl.ds(half, half), 1 - y], chip(x, 1 - y, z)
-        return far_copy(src, recv1.at[g, b], s1.at[g, b], r1.at[g, b], to)
-
-    def send2(g, b):
-        zs = pl.ds(b * half, half)
+            src, to = G.at[g, pl.ds(half, half), 1 - y, :, :, cs], chip(x, 1 - y, z)
+        dst = recv1.at[g, b, :, :, :, cs]
+        return far_copy(src, dst, s1.at[v, b], r1.at[v, b], to)
+
+    def send2(v, b):
+        g, cs = place(v)
+        at = pl.ds(b * half, half)
         if b == 0:
-            src, to = G.at[g, zs, 1 - y, x], chip(x, 1 - y, z)
+            src, to = G.at[g, at, 1 - y, x, :, cs], chip(x, 1 - y, z)
         else:
-            src, to = G.at[g, zs, y, 1 - x], chip(1 - x, y, z)
-        return far_copy(src, recv2.at[g, zs], s2.at[g, b], r2.at[g, b], to)
-
-    def send3(g, d):
+            src, to = G.at[g, at, y, 1 - x, :, cs], chip(1 - x, y, z)
+        dst = recv2.at[g, at, :, cs]
+        return far_copy(src, dst, s2.at[v, b], r2.at[v, b], to)
+
+    def send3(v, d):
+        g, cs = place(v)
         to = lax.rem(z + d, zc)
-        return far_copy(
-            G.at[g, to, y, x], recv3.at[g, d - 1], s3.at[g, d - 1], r3.at[g, d - 1], chip(x, y, to)
-        )
-
-    def stage1(g):
+        src, dst = G.at[g, to, y, x, :, cs], recv3.at[g, d - 1, :, cs]
+        return far_copy(src, dst, s3.at[v, d - 1], r3.at[v, d - 1], chip(x, y, to))
+
+    def start1(v):
+        if use_rs:
+            for b in range(2):
+                send1(v, b).start()
+
+    def stage1(v):
+        g, cs = place(v)
         for b in range(2):
-            send1(g, b).wait_recv()
+            send1(v, b).wait_recv()
 
             def body(k, b=b):
                 for j in range(2):
-                    at = G.at[g, k, j, x] if b == 0 else G.at[g, half + k, y, j]
-                    at[...] = (at[...].astype(f32) + recv1[g, b, k, j].astype(f32)).astype(bf16)
+                    at = G.at[g, k, j, x, :, cs] if b == 0 else G.at[g, half + k, y, j, :, cs]
+                    got = recv1[g, b, k, j, :, cs]
+                    at[...] = (at[...].astype(f32) + got.astype(f32)).astype(bf16)
 
             loop(half, body)
-            send2(g, b).start()
-
-    def stage2(g):
+            send2(v, b).start()
+
+    def stage2(v):
+        g, cs = place(v)
         for b in range(2):
-            send2(g, b).wait_recv()
+            send2(v, b).wait_recv()
 
         def body(k):
-            at = G.at[g, k, y, x]
-            at[...] = (at[...].astype(f32) + recv2[g, k].astype(f32)).astype(bf16)
+            at = G.at[g, k, y, x, :, cs]
+            at[...] = (at[...].astype(f32) + recv2[g, k, :, cs].astype(f32)).astype(bf16)
 
         loop(zc, body)
         for d in range(1, zc):
-            send3(g, d).start()
+            send3(v, d).start()
 
     def final(g):
-        for d in range(1, zc):
-            send3(g, d).wait_recv()
+        if g in z_first:
+            total = G[g, z, y, x].astype(f32)
+            for k in range(3):
+                plane_copy(g, k).wait_recv()
+                total = total + recv2[g, k].astype(f32)
+            return total
+        for v in range(g, g + runs if g == last else g + 1):
+            for d in range(1, zc):
+                send3(v, d).wait_recv()
         total = G[g, z, y, x].astype(f32)
         for d in range(1, zc):
             total = total + recv3[g, d - 1].astype(f32)
         return total
 
-    def start1(g):
-        if use_rs:
-            for b in range(2):
-                send1(g, b).start()
-
+    z_first = (fgroups // 2, 2 * fgroups - 1)
+    others = [v for v in range(last + runs) if v not in z_first]
     ahead = 3
 
     def tick(i):
         if not use_rs:
             return
-        if i < groups:
-            stage1(i)
-            if i + ahead < groups:
-                start1(i + ahead)
-        if 1 <= i <= groups:
-            stage2(i - 1)
+        if i < len(others):
+            stage1(others[i])
+            if i + ahead < len(others):
+                start1(others[i + ahead])
+        if 1 <= i <= len(others):
+            stage2(others[i - 1])
+
+    end = (z == 0) | (z == 3)
+    near_middle = jnp.where(z == 0, 1, 2)
+    near_end = jnp.where(z == 1, 0, 3)
+    lowest = jnp.where((z == 0) | (z == 1), 1, 0)
+
+    def z_copy(g, k):
+        q = z_first.index(g)
+        src, slot, to = (
+            (G.at[g, pl.ds(lowest, 2)], recv1.at[g], near_middle),
+            (G.at[g, near_end], zr.at[q, 0], near_end),
+            (G.at[g, 3 - z], zr.at[q, 1], 3 - z),
+            (G.at[g, 3 - near_end], zr.at[q, 1], 3 - near_end),
+            (G.at[g, lowest + 2], zr.at[q, 0], near_middle),
+        )[k]
+        return far_copy(src, slot, zs.at[q, k], zw.at[q, k], chip(x, y, to))
+
+    def plane_copy(g, k):
+        q = z_first.index(g)
+        cx, cy = ((1 - x, y), (x, 1 - y), (1 - x, 1 - y))[k]
+        return far_copy(
+            G.at[g, z, cy, cx],
+            recv2.at[g, k],
+            zs.at[q, 5 + k],
+            zw.at[q, 5 + k],
+            chip(cx, cy, z),
+        )
+
+    def z_begin(g):
+        if not use_rs:
+            return
+
+        @pl.when(end)
+        def _():
+            z_copy(g, 0).start()
+            z_copy(g, 4).start()
+
+        @pl.when(jnp.logical_not(end))
+        def _():
+            z_copy(g, 1).start()
+
+    def z_middle(g):
+        if not use_rs:
+            return
+        q = z_first.index(g)
+
+        @pl.when(jnp.logical_not(end))
+        def _():
+            z_copy(g, 0).wait_recv()
+            z_copy(g, 4).wait_recv()
+
+            def body(j):
+                for k in range(2):
+                    for at, got in (
+                        (G.at[g, lowest, j, k], recv1[g, 0, j, k]),
+                        (G.at[g, lowest + 1, j, k], recv1[g, 1, j, k]),
+                        (G.at[g, lowest + 2, j, k], zr[q, 0, j, k]),
+                    ):
+                        at[...] = (at[...].astype(f32) + got.astype(f32)).astype(bf16)
+
+            loop(2, body)
+            z_copy(g, 2).start()
+            z_copy(g, 3).start()
+
+    def z_end(g):
+        if not use_rs:
+            return
+        q = z_first.index(g)
+
+        @pl.when(end)
+        def _():
+            z_copy(g, 1).wait_recv()
+            z_copy(g, 3).wait_recv()
+
+            def body(j):
+                for k in range(2):
+                    at = G.at[g, z, j, k]
+                    at[...] = (
+                        at[...].astype(f32) + zr[q, 0, j, k].astype(f32) + zr[q, 1, j, k].astype(f32)
+                    ).astype(bf16)
+
+            loop(2, body)
+
+        @pl.when(jnp.logical_not(end))
+        def _():
+            z_copy(g, 2).wait_recv()
+
+            def body(j):
+                for k in range(2):
+                    at = G.at[g, z, j, k]
+                    at[...] = (at[...].astype(f32) + zr[q, 1, j, k].astype(f32)).astype(bf16)
+
+            loop(2, body)
+
+        for k in range(3):
+            plane_copy(g, k).start()
+
+    def z_sent(g):
+        @pl.when(end)
+        def _():
+            z_copy(g, 0).wait_send()
+            z_copy(g, 4).wait_send()
+
+        @pl.when(jnp.logical_not(end))
+        def _():
+            for k in range(1, 4):
+                z_copy(g, k).wait_send()
+
+        for k in range(3):
+            plane_copy(g, k).wait_send()
 
     RT = 128
 
@@ -359,6 +495,7 @@
         inv = lax.rsqrt(var + norm_eps)
         return (resid_tile - mean) * inv, inv
 
+    mixed_peer = qkv_peer.at[:, pl.ds(2 * DH, DH)]
     dctx = outb = hbf
 
     def turned(k, sem, i):
@@ -408,13 +545,10 @@
         def body(at):
             u = mm(hbf[...], wup[:, at]) + pf[pl.ds(0, 1), at]
             u2 = u * u
-            half = 0.5 * jnp.tanh(u * (0.7978845608 + (0.7978845608 * 0.044715) * u2)) + 0.5
-            act[:, at] = (u * half * pf[pl.ds(unit_row, 1), at]).astype(bf16)
+            t = jnp.tanh(u * (0.7978845608 + (0.7978845608 * 0.044715) * u2))
+            act[:, at] = ((u * (0.5 * pf[pl.ds(unit_row, 1), at])) * (1.0 + t)).astype(bf16)
             if keep:
-                slope = half + u * (2.0 * half * (1.0 - half)) * (
-                    0.7978845608 + (3.0 * 0.7978845608 * 0.044715) * u2
-                )
-                gp[:, at] = slope.astype(bf16)
+                gp[:, at] = u.astype(bf16)
 
         tiles(F, body)
 
@@ -453,36 +587,48 @@
     for i in (1, 2, 3):
         local[i].wait()
     project_in(h * DH)
-    for i in (1, 2, 3, 8, 9):
-        remote[i].wait_recv()
-    project_in(oh * DH)
-
-    loop(M // 128, lambda i: turn(tok[pl.ds(al(i * 128, 128), 128), :], X_TOK, 0, i))
+
 
     lane = lax.broadcasted_iota(jnp.int32, (1, 2 * HEAD), 1)
     head_mask = [(lane < HEAD).astype(bf16), (lane >= HEAD).astype(bf16)]
 
-    QT = 512
+    QT = M
+
+    own_pairs = pairs // 2
 
     def attend(i):
-        p = lax.div(i, M // QT)
-        rows = pl.ds(al(lax.rem(i, M // QT) * QT, QT), QT)
+        @pl.when(i == own_pairs)
+        def _():
+            for k in (1, 2, 3, 8, 9):
+                remote[k].wait_recv()
+            project_in(oh * DH)
+
+        p = lax.rem(h * own_pairs + i, pairs)
+        rows = pl.ds(0, QT)
         at = pl.ds(al(p * 128, 128), 128)
         q2 = qkv[rows, at]
         k2 = qkv[:, pl.ds(al(p * 128 + D, 128), 128)]
         v2 = qkv[:, pl.ds(al(p * 128 + 2 * D, 128), 128)]
         total = None
+        inverse = []
         for b in range(2):
             s = mm_nt(q2 * head_mask[b], k2) + bias[rows, :].astype(f32)
             e = jnp.exp(s - jnp.max(s, -1, keepdims=True))
-            w = (e * (1.0 / jnp.sum(e, -1, keepdims=True))).astype(bf16)
+            w = e.astype(bf16)
             probs[2 * p + b, rows] = w
             part = mm(w, v2 * head_mask[b])
+            inverse.append(1.0 / jnp.sum(e, -1, keepdims=True))
             total = part if total is None else total + part
+        total = total * jnp.where(lane < HEAD, inverse[0], inverse[1])
+        keep_ref[rows, :] = jnp.where(
+            lane == 2 * p + 1,
+            inverse[0],
+            jnp.where(lane == 2 * p + 2, inverse[1], keep_ref[rows, :]),
+        )
         ctx[rows, at] = total.astype(bf16)
         mixed[rows, at] = (total * pd[pl.ds(PZHEAD, 1), at]).astype(bf16)
 
-    loop(pairs * (M // QT), attend)
+    loop(pairs, attend)
     mixed_copy = to_peer(4, mixed.at[:, ocols], mixed_peer)
 
     fed(4)
@@ -523,7 +669,13 @@
         da = mm_nt(dbf[...], wdown[at, :])
         su = jnp.sum((da * act[:, at].astype(f32)).reshape(M // 8, 8, NT), axis=0)
         vf[pl.ds(8, 8), at] = su
-        du = (da * pf[pl.ds(1, 1), at] * gp[:, at].astype(f32)).astype(bf16)
+        u = gp[:, at].astype(f32)
+        u2 = u * u
+        t = jnp.tanh(u * (0.7978845608 + (0.7978845608 * 0.044715) * u2))
+        slope = (1.0 + t) * (
+            1.0 + (u * (1.0 - t)) * (0.7978845608 + (3.0 * 0.7978845608 * 0.044715) * u2)
+        )
+        du = (da * (0.5 * pf[pl.ds(1, 1), at]) * slope).astype(bf16)
         gp[:, at] = du
         vf[pl.ds(0, 8), at] = jnp.sum(du.astype(f32).reshape(M // 8, 8, NT), axis=0)
 
@@ -562,8 +714,9 @@
     start1(0)
     start1(1)
     down_grad(1)
-    start1(2)
-    pl.semaphore_signal(credit, inc=1, device_id=peer, device_id_type=MESH)
+    z_begin(2)
+    start1(3)
+    pl.semaphore_signal(credit.at[0], inc=1, device_id=peer, device_id_type=MESH)
 
     loop(F // NT - early, lambda i: dactive_tile(pl.ds(al((i + early) * NT, NT), NT)))
     dup_copy = to_peer(7, gp.at[:, ofcols], dup_peer)
@@ -572,7 +725,6 @@
         acc[:, at] = mm_nt(gp[...], wup[at, :])
 
     tiles(D, dhidden_tile)
-    tick(0)
 
     turned_in(X_HID, 1)
     dup_copy.wait_recv()
@@ -585,12 +737,15 @@
             lambda: dup_peer[:, pl.ds(al(i * D, 128), D)],
         )
 
-    loop(fgroups // 2, up_grad)
+    up_grad(0)
+    tick(0)
+    up_grad(1)
+    pl.semaphore_signal(credit.at[1], inc=1, device_id=peer, device_id_type=MESH)
 
     out_near.wait()
     out_far.wait_send()
     turned_out(X_DDOWN, 2)
-    pl.semaphore_wait(credit, 1)
+    pl.semaphore_wait(credit.at[0], 1)
 
     def first_norm_back(i, at):
         value = resid[at, :]
@@ -609,23 +764,36 @@
         dbf[at, :] = branch_grad
         turn(branch_grad, X_DBR, 3, i)
 
+    z_begin(7)
     tick(1)
     row_loop(first_norm_back)
-    def dmixed_tile(at):
+    def dmixed_tile(i):
+        at = pl.ds(i * NT, NT)
         dm = mm_nt(dbf[...], wout[at, :])
         vd[pl.ds(8 * S_ZHEAD, 8), at] = jnp.sum(
             (dm * ctx[:, at].astype(f32)).reshape(M // 8, 8, NT), axis=0
         )
-        dctx[:, at] = (dm * pd[pl.ds(PZHEAD, 1), at]).astype(bf16)
-
-    tiles(D, dmixed_tile)
+        first = 1 + i * (NT // HEAD)
+        inverse = jnp.concatenate(
+            [
+                jnp.where(lane < HEAD, keep_ref[:, k : k + 1], keep_ref[:, k + 1 : k + 2])
+                for k in range(first, first + NT // HEAD, 2)
+            ],
+            axis=1,
+        )
+        dctx[:, at] = (dm * pd[pl.ds(PZHEAD, 1), at] * inverse).astype(bf16)
+
+    for i in range(D // NT):
+        dmixed_tile(i)
+    turned_out(X_HID, 1)
+    pl.semaphore_wait(credit.at[1], 1)
+    loop(M // 128, lambda i: turn(tok[pl.ds(al(i * 128, 128), 128), :], X_TOK, 0, i))
     turned_in(X_DBR, 3)
     mixed_copy.wait_recv()
     g_out = 2 * fgroups
     grad_group(g_out, X_DBR, lambda: mixed[:, cols], lambda: mixed_peer[...])
     tick(2)
-
-    own_pairs = pairs // 2
+    z_middle(2)
 
     def send_pair(j, t):
         return far_copy(
@@ -651,13 +819,13 @@
             rows = pl.ds(t * 256, 256)
             q2, c2 = qkv[rows, qa], dctx[rows, qa]
             dq = None
+            shared = c2.astype(f32) * ctx[rows, qa].astype(f32)
             for b in range(2):
                 m = head_mask[b]
                 w = probs[2 * p + b, rows]
-                wf = w.astype(f32)
                 dp = mm_nt(c2 * m, v2)
-                delta = jnp.sum(wf * dp, -1, keepdims=True)
-                ds = (wf * (dp - delta)).astype(bf16)
+                delta = jnp.sum(shared * m.astype(f32), -1, keepdims=True)
+                ds = (w.astype(f32) * (dp - delta)).astype(bf16)
                 a = mm(ds, k2 * m)
                 bb = mm((q2 * m).T, ds)
                 c = mm((c2 * m).T, w)
@@ -692,7 +860,7 @@
                 lambda: qkv_peer[:, pl.ds(al(j * DH, 128), DH)],
             )
 
-        for at_step, k in ((2, 3), (5, 4)):
+        for at_step, k in ((1, 3), (4, 4)):
 
             @pl.when(i == at_step)
             def _(k=k):
@@ -744,6 +912,8 @@
             copy.start()
             plane.append(copy)
     tick(5)
+    z_end(2)
+    z_middle(7)
 
     in_near.wait()
     in_far.wait_send()
@@ -751,7 +921,6 @@
     mixed[...] = (ctx[...].astype(f32) * par(PHHEAD)).astype(bf16)
     project_out(1.0, PHG1, PHS1, False)
     act_copy.wait_send()
-    tick(6)
     zsum = []
     if use_rs:
         for copy in plane:
@@ -765,9 +934,10 @@
             copy.start()
             zsum.append(copy)
     up(2, False)
+    tick(6)
+    down()
     tick(7)
-    down()
-    tick(8)
+    z_end(7)
 
     def hard_norm(i, at):
         xh1, inv1 = normed(resid[at, :])
@@ -791,23 +961,34 @@
     err_copy = far_copy(send_err, recv_err, xs.at[17], xr.at[17], peer)
     err_copy.start()
 
-    for i in range(9, groups + 1):
-        tick(i)
-    if use_rs:
-        pr = D // n
-        grads = []
-        for g in range(groups):
-            at = acc.at[pl.ds((g // 2) * pr, pr), pl.ds((g % 2) * DH, DH)]
+    grads = []
+
+    def finish(*which):
+        if not use_rs:
+            return
+        for g in which:
+            at = acc.at[pl.ds((g // 2) * (D // n), D // n), pl.ds((g % 2) * DH, DH)]
             at[...] = final(g)
             copy = pltpu.make_async_copy(at, grads_out.at[g], lsem.at[13 + g])
             copy.start()
             grads.append(copy)
+
+    if use_rs:
+        tick(8)
         for copy in zsum:
             copy.wait_recv()
         total = packs[4]
         for d in range(1, zc):
             total = total + packs[4 + d]
         vec_out[...] = total
+        finish(*(v for v in others[:6]))
+        tick(9)
+        finish(z_first[0], others[6])
+        tick(10)
+        finish(others[7], z_first[1])
+        for i in range(11, len(others) + 1):
+            tick(i)
+        finish(last - 1, last)
     else:
         vec_out[...] = packs[0]
         grads_near = pltpu.make_async_copy(G, grads_out, lsem.at[13])
@@ -825,7 +1006,6 @@
     for copy in remote:
         copy.wait_send()
     turned_out(X_TOK, 0)
-    turned_out(X_HID, 1)
     turned_out(X_DBR, 3)
     dup_copy.wait_send()
     for j in range(own_pairs):
@@ -836,7 +1016,9 @@
             copy.wait()
         for copy in plane + zsum:
             copy.wait_send()
-        for g in range(groups):
+        for g in z_first:
+            z_sent(g)
+        for g in others:
             for b in range(2):
                 send1(g, b).wait_send()
                 send2(g, b).wait_send()
@@ -883,7 +1065,7 @@
     F = 2 * FH
     blocks, M = segment_ids.shape
     n = rows
-    use_rs = n % 8 == 0 and D % n == 0 and (D // n) % 16 == 0
+    use_rs = n == 16 and D % n == 0 and (D // n) % 16 == 0
     groups = 4 + 2 * (FH // DH)
     fgroups = FH // DH
     zc = n // 4
@@ -903,11 +1085,12 @@
     if use_rs:
         out_shape += [shape((groups, pr, DH), f32)]
         gshape = (groups, zc, 2, 2, pr, DH)
+        r4 = (2, 2, 2, 2, pr, DH)
         r1, r2, r3 = (groups, 2, zc // 2, 2, pr, DH), (groups, zc, pr, DH), (groups, zc - 1, pr, DH)
     else:
         out_shape += [shape((groups, D, DH), bf16)]
         gshape = (groups, D, DH)
-        r1 = r2 = r3 = (1, 16, 128)
+        r1 = r2 = r3 = r4 = (1, 16, 128)
     dma = pltpu.SemaphoreType.DMA
     V = pltpu.VMEM
     scratch = [
@@ -925,7 +1108,6 @@
         V((D // HEAD, M, M), bf16),
         V((M, D), bf16),
         V((M, D), bf16),
-        V((M, DH), bf16),
         V((M, D), f32),
         V((M, D), bf16),
         V((M, D), f32),
@@ -935,7 +1117,7 @@
         V((M, FH), bf16),
         V((M, D), f32),
         V((M, D), bf16),
-        V((3, D, 2 * M), bf16),
+        V((2, D, 2 * M), bf16),
         V((16 * 8, D), f32),
         V((16, F), f32),
         V((2, 24, DH), f32),
@@ -951,13 +1133,16 @@
         dma((10,)),
         dma((48 + zc,)),
         dma((48 + zc,)),
-        dma((groups, 2)),
-        dma((groups, 2)),
-        dma((groups, 2)),
-        dma((groups, 2)),
-        dma((groups, zc - 1)),
-        dma((groups, zc - 1)),
-        pltpu.SemaphoreType.REGULAR,
+        dma((groups + DH // 128 - 1, 2)),
+        dma((groups + DH // 128 - 1, 2)),
+        dma((groups + DH // 128 - 1, 2)),
+        dma((groups + DH // 128 - 1, 2)),
+        dma((groups + DH // 128 - 1, zc - 1)),
+        dma((groups + DH // 128 - 1, zc - 1)),
+        V(r4, bf16),
+        dma((2, 8)),
+        dma((2, 8)),
+        pltpu.SemaphoreType.REGULAR((2,)),
     ]
     results = pl.pallas_call(
         functools.partial(layer_kernel, (n, D, F, M, use_rs)),
@@ -1143,7 +1328,7 @@
         far.wait()
 
 
-VMEM_LIMIT = 64 * 1024 * 1024 - 256 * 1024
+VMEM_LIMIT = 64 * 1024 * 1024 - 64 * 1024
 
 
 def solution(mesh):

time: 125 us -> 117 us (0.936)
  Pallas kernels: 123 us -> 116 us
    pallas_call x1, Pallas kernels: 118 us -> 111 us  [shards(): pl.pallas_call(functools.partial(layer_kernel, (n, D, F, M, use_rs)), out...]
where the time goes in v3:
time: 117 us
  Pallas kernels  116 us (99%)
    pallas_call x1, Pallas kernels, shards(): pl.pallas_call(functools.partial(layer_kernel, (n, D, F, M, use_rs)), out...  111 us
    pallas_call x1, Pallas kernels, shards(): pl.pallas_call(functools.partial(finish_kernel, fgroups), out_shape=[shap...  5.01 us

profile of v3, /device:TPU:0, one launch (start us, length us, event | category | flops | bytes accessed | tf_op | source)
XLA Modules:
  0.0 116.8 jit_solution(5481071753145237947)
XLA Ops:
  0.7 110.9 %shard_map.461 = (bf16[1024,384]{1,0:T(8,128)(2,1)}, f32[1024,384]{1,0:T(8,128)}, bf16[1024,384]{1,0:T(8,128)(2,1)}, f32[2,512]{1,0:T(2,128)}, f32[24,384]{1,0:T(8,128)}, /*index=5*/f32[12,48,384]{2,1,0:T(8,128)}) custom-call(bf16[1024,384]{1,0:T(8,128)(2,1)} %refs_0_.1, bf16[1024,384]{1,0:T(8,128)(2,1)} %refs_1_.1, s32[2,512]{1,0:T(2,128)} %refs_2_.1, ...), custom_call_target="tpu_custom_call" | custom-call | tf_op jit(solution)/shard_map/pallas_call | solution.py:1147
  111.6 5.0 %shard_map.462 = (bf16[1024,384]{1,0:T(8,128)(2,1)}, f32[1024,384]{1,0:T(8,128)}, f32[48,384]{1,0:T(8,128)}, f32[384]{0:T(512)}, f32[48,384]{1,0:T(8,128)}, /*in...) custom-call(bf16[1024,384]{1,0:T(8,128)(2,1)} %get-tuple-element.52., ...), custom_call_target="tpu_custom_call" | custom-call | tf_op jit(solution)/shard_map/pallas_call | solution.py:1198

commit v4 on v3

--- a/solution.py
+++ b/solution.py
@@ -480,7 +480,8 @@
     RT = 128
 
     def row_loop(body):
-        loop(M // RT, lambda i: body(i, pl.ds(al(i * RT, RT), RT)))
+        for i in range(M // RT):
+            body(i, pl.ds(i * RT, RT))
 
     def add_sum(k, value):
         at = vd.at[pl.ds(8 * k, 8)]
@@ -522,7 +523,11 @@
     NT = 256
 
     def tiles(count, body):
-        loop(count // NT, lambda i: body(pl.ds(al(i * NT, NT), NT)))
+        if count == D:
+            for i in range(count // NT):
+                body(pl.ds(i * NT, NT))
+        else:
+            loop(count // NT, lambda i: body(pl.ds(al(i * NT, NT), NT)))
 
     def project_out(gate, gain, shift, keep):
         def body(at):
@@ -767,6 +772,7 @@
     z_begin(7)
     tick(1)
     row_loop(first_norm_back)
+    z_middle(2)
     def dmixed_tile(i):
         at = pl.ds(i * NT, NT)
         dm = mm_nt(dbf[...], wout[at, :])
@@ -793,7 +799,6 @@
     g_out = 2 * fgroups
     grad_group(g_out, X_DBR, lambda: mixed[:, cols], lambda: mixed_peer[...])
     tick(2)
-    z_middle(2)
 
     def send_pair(j, t):
         return far_copy(
@@ -868,6 +873,8 @@
 
     turned_in(X_TOK, 0)
     loop(pairs, attend_back)
+    z_end(2)
+    z_middle(7)
 
     hidden_sum = 0.0
     for shift_row, gain_row, gain, shift in ((S_S1, S_G1, PG1, PS1), (S_S2, S_G2, PG2, PS2)):
@@ -912,8 +919,6 @@
             copy.start()
             plane.append(copy)
     tick(5)
-    z_end(2)
-    z_middle(7)
 
     in_near.wait()
     in_far.wait_send()

time: 117 us -> 115 us (0.983)
  Pallas kernels: 116 us -> 114 us
    pallas_call x1, Pallas kernels: 111 us -> 109 us  [shards(): pl.pallas_call(functools.partial(layer_kernel, (n, D, F, M, use_rs)), out...]
where the time goes in v4:
time: 115 us
  Pallas kernels  114 us (99%)
    pallas_call x1, Pallas kernels, shards(): pl.pallas_call(functools.partial(layer_kernel, (n, D, F, M, use_rs)), out...  109 us
    pallas_call x1, Pallas kernels, shards(): pl.pallas_call(functools.partial(finish_kernel, fgroups), out_shape=[shap...  5.01 us

profile of v4, /device:TPU:0, one launch (start us, length us, event | category | flops | bytes accessed | tf_op | source)
XLA Modules:
  0.0 114.6 jit_solution(18158476608370351132)
XLA Ops:
  0.7 108.7 %shard_map.461 = (bf16[1024,384]{1,0:T(8,128)(2,1)}, f32[1024,384]{1,0:T(8,128)}, bf16[1024,384]{1,0:T(8,128)(2,1)}, f32[2,512]{1,0:T(2,128)}, f32[24,384]{1,0:T(8,128)}, /*index=5*/f32[12,48,384]{2,1,0:T(8,128)}) custom-call(bf16[1024,384]{1,0:T(8,128)(2,1)} %refs_0_.1, bf16[1024,384]{1,0:T(8,128)(2,1)} %refs_1_.1, s32[2,512]{1,0:T(2,128)} %refs_2_.1, ...), custom_call_target="tpu_custom_call" | custom-call | tf_op jit(solution)/shard_map/pallas_call | solution.py:1152
  109.4 5.0 %shard_map.462 = (bf16[1024,384]{1,0:T(8,128)(2,1)}, f32[1024,384]{1,0:T(8,128)}, f32[48,384]{1,0:T(8,128)}, f32[384]{0:T(512)}, f32[48,384]{1,0:T(8,128)}, /*in...) custom-call(bf16[1024,384]{1,0:T(8,128)(2,1)} %get-tuple-element.52., ...), custom_call_target="tpu_custom_call" | custom-call | tf_op jit(solution)/shard_map/pallas_call | solution.py:1203
